TPU v7x, 32 devices: a whole 2x2x4 slice. The times are simulated.
32 devices in a mesh: parts: 2 (over x), row: 16 (over z, y, core).
Axes of the slice: x: 2, y: 2, z: 4, core: 2. Of those that a mesh axis runs over, the one named last changes fastest.
Arguments:
- latent: bfloat16 [64, 256, 512], P(('parts', 'row')), parts along dimension 0, may hold values from -6 to 6
- conv_first: bfloat16 [3, 3, 512, 512], P(None, None, 'row'), may hold values from -0.09375 to 0.09375
- conv_second: bfloat16 [3, 3, 512, 512], P(None, None, 'row'), may hold values from -0.09375 to 0.09375
- w_query: bfloat16 [512, 512], replicated
- w_key: bfloat16 [512, 512], replicated
- w_value: bfloat16 [512, 512], replicated, may hold values from -0.25 to 0.25
- w_out: bfloat16 [512, 512], replicated, may hold values from -0.25 to 0.25
- w_in: bfloat16 [512, 2048], replicated, may hold values from -0.25 to 0.25
- w_down: bfloat16 [2048, 512], replicated, may hold values from -0.125 to 0.125
- conv_up: bfloat16 [3, 3, 512, 512], P(None, None, 'row'), may hold values from -0.09375 to 0.09375
Outputs:
- latent_out: bfloat16 [64, 256, 512], P(('parts', 'row')), parts along dimension 0
- upsampled: bfloat16 [64, 256, 512], P('parts', 'row'), parts along dimension 0
There are 2 independent parts, one for each index of `parts`. A program takes and returns all parts, laid end to end along the dimension named above; an argument that names none is the same for every part. Nothing has to cross between parts.
All inputs are finite; a program needn't handle non-finite values.
Results may differ from a plain program's by a relative error of at most 0.015.
Values may be sent and summed in bfloat16 or wider, within the bound.
A program may use at most 128 MiB of HBM per device.

v0:
```python
import jax
import jax.numpy as jnp
from jax import lax
from jax.sharding import PartitionSpec as P

HD = 64
GRID = 16


def padded_2(value, sides, width):
    for axis, dim in sides:
        size, length = (lax.axis_size(axis), value.shape[dim])
        up = [(i, (i + 1) % size) for i in range(size - 1)]
        down = [(j, i) for i, j in up]
        last = lax.slice_in_dim(value, length - width, length, axis=dim)
        initial = lax.slice_in_dim(value, 0, width, axis=dim)
        before = lax.ppermute(last, axis, up)
        after = lax.ppermute(initial, axis, down)
        value = jnp.concatenate([before, value, after], axis=dim)
    return value


def rms_round(values):
    meansq = jnp.mean(values * values, axis=-1, keepdims=True)
    return (values * lax.rsqrt(meansq + 1e-06)).astype(jnp.bfloat16)


def softmax_round(scores):
    highest = jnp.max(scores, axis=-1, keepdims=True)
    lifted = jnp.exp(scores - highest)
    return (lifted / jnp.sum(lifted, axis=-1, keepdims=True)).astype(jnp.bfloat16)


def whole_kernel(kernel_piece):
    return lax.all_gather(kernel_piece, "row", axis=2, tiled=True)


def convolve(padded, kernel, out_rows, out_cols):
    tap_stack = jnp.stack(
        [
            padded[shift_row : shift_row + out_rows, shift_col : shift_col + out_cols]
            for shift_row in range(3)
            for shift_col in range(3)
        ],
        axis=2,
    )
    in_chans = tap_stack.shape[3]
    return jnp.dot(
        tap_stack.reshape(-1, 9 * in_chans),
        kernel.reshape(9 * in_chans, kernel.shape[3]),
        preferred_element_type=jnp.float32,
    )


def on_device(
    latent, conv_first, conv_second, w_query, w_key, w_value, w_out, w_in, w_down, conv_up
):
    devices = lax.axis_size("row")
    grid_rows, grid_cols, channels = latent.shape
    first_kernel, second_kernel, up_kernel = (conv_first, conv_second, conv_up)
    current = latent
    for kernel in (first_kernel, second_kernel):
        active = jax.nn.gelu(current.astype(jnp.float32)).astype(jnp.bfloat16)
        padded = padded_2(active, (("row", 0),), 1)
        padded = jnp.pad(padded, ((0, 0), (1, 1), (0, 0)))
        kernel = whole_kernel(kernel)
        mixing = convolve(padded, kernel, grid_rows, grid_cols)
        current = (
            current.astype(jnp.float32) + mixing.reshape(grid_rows, grid_cols, channels)
        ).astype(jnp.bfloat16)
    normed = rms_round(current.astype(jnp.float32)).reshape(-1, channels)
    send_shape = (grid_rows, GRID, devices, -1)
    queries = (
        jnp.dot(normed, w_query, preferred_element_type=jnp.float32)
        .astype(jnp.bfloat16)
        .reshape(send_shape)
    )
    keys_local = (
        jnp.dot(normed, w_key, preferred_element_type=jnp.float32)
        .astype(jnp.bfloat16)
        .reshape(send_shape)
    )
    values_local = (
        jnp.dot(normed, w_value, preferred_element_type=jnp.float32)
        .astype(jnp.bfloat16)
        .reshape(send_shape)
    )
    query_win, key_win, value_win = (
        lax.all_to_all(queries, "row", split_axis=2, concat_axis=0, tiled=True),
        lax.all_to_all(keys_local, "row", split_axis=2, concat_axis=0, tiled=True),
        lax.all_to_all(values_local, "row", split_axis=2, concat_axis=0, tiled=True),
    )
    all_rows = query_win.shape[0]
    band_rows = all_rows // GRID
    per_heads = query_win.shape[3] // HD
    window_shape = (GRID, band_rows, GRID, per_heads, HD)
    scores = jnp.einsum(
        "arbhd,erfhd->rhabef",
        query_win.reshape(window_shape),
        key_win.reshape(window_shape),
        preferred_element_type=jnp.float32,
    ) * HD ** (-0.5)
    scores = scores.reshape(band_rows, per_heads, GRID * GRID, GRID * GRID)
    probs = softmax_round(scores).reshape(band_rows, per_heads, GRID, GRID, GRID, GRID)
    attended = jnp.einsum(
        "rhabef,erfhd->arbhd",
        probs,
        value_win.reshape(window_shape),
        preferred_element_type=jnp.float32,
    )
    attended = attended.astype(jnp.bfloat16).reshape(all_rows, GRID, 1, -1)
    returned = lax.all_to_all(attended, "row", split_axis=0, concat_axis=2, tiled=True).reshape(
        -1, channels
    )
    projected = jnp.dot(returned, w_out, preferred_element_type=jnp.float32).reshape(
        grid_rows, grid_cols, channels
    )
    current = (current.astype(jnp.float32) + projected).astype(jnp.bfloat16)
    normed_two = rms_round(current.astype(jnp.float32)).reshape(-1, channels)
    hidden = jax.nn.gelu(jnp.dot(normed_two, w_in, preferred_element_type=jnp.float32)).astype(
        jnp.bfloat16
    )
    lowered = jnp.dot(hidden, w_down, preferred_element_type=jnp.float32).reshape(
        grid_rows, grid_cols, channels
    )
    latent_out = (current.astype(jnp.float32) + lowered).astype(jnp.bfloat16)
    central = latent_out[:, grid_cols // 4 : 3 * grid_cols // 4]
    central_cols = central.shape[1]
    slice_cols = central_cols // devices
    padded_central = jnp.pad(central, ((0, 0), (1, 1), (0, 0)))
    left_part = padded_central[:, :central_cols].reshape(grid_rows, devices, slice_cols, channels)
    first_extra = padded_central[:, slice_cols::slice_cols]
    second_extra = padded_central[:, slice_cols + 1 :: slice_cols]
    outgoing = jnp.concatenate(
        [left_part, first_extra[:, :, None], second_extra[:, :, None]], axis=2
    )
    arrived = lax.all_to_all(outgoing, "row", split_axis=1, concat_axis=0, tiled=True)
    total_rows = arrived.shape[0]
    framed = arrived[total_rows // 4 : 3 * total_rows // 4, 0]
    doubled = jnp.repeat(jnp.repeat(framed, 2, axis=0), 2, axis=1)[:, 1:-1]
    doubled = jnp.pad(doubled, ((1, 1), (0, 0), (0, 0)))
    out_cols = 2 * slice_cols
    up_kernel = whole_kernel(up_kernel)
    upsampled = (
        convolve(doubled, up_kernel, total_rows, out_cols)
        .reshape(total_rows, out_cols, channels)
        .astype(jnp.bfloat16)
    )
    return (latent_out, upsampled)


def solution(mesh):
    placed = (
        P(("parts", "row"), None, None),
        P(None, None, "row", None),
        P(None, None, "row", None),
        P(),
        P(),
        P(),
        P(),
        P(),
        P(),
        P(None, None, "row", None),
    )
    return jax.shard_map(
        on_device,
        mesh=mesh,
        in_specs=placed,
        out_specs=(P(("parts", "row"), None, None), P("parts", "row", None)),
        check_vma=False,
    )
```

profile of v0, /device:TPU:9, one launch (start us, length us, event | category | flops | bytes accessed | tf_op | source)
XLA Modules:
  0.0 309.5 jit_solution(8963559756864305286)
XLA Ops:
  10.1 3.7 %collective-permute-start = (bf16[1,256,512]{2,1,0:T(8,128)(2,1)S(1)}, bf16[1,256,512]{2,1,0:T(8,128)(2,1)S(1)}, u32[]{:S(2)}, u32[]{:S(2)}) collective-permute-start(bf16[1,256,512]{2,1,0:T(8,128)(2,1)S(1)} %get-tuple-element.4), channel_id=1, source_target_pairs={{0,1},{1,2},{2,3},{3,4},{4,5},{5,6},{6,7},{7,8},{8,9},{9,10},{10,1... | collective-permute-start | bytes 786440 | tf_op jit(solution)/shard_map/ppermute | solution.py:17
  13.8 1.9 collective-permute-start.1
  17.1 4.4 %collective-permute-done.1 = bf16[1,256,512]{2,1,0:T(8,128)(2,1)S(1)} collective-permute-done((bf16[1,256,512]{2,1,0:T(8,128)(2,1)S(1)}, bf16[1,256,512]{2,1,0:T(8,128)(2,1)S(1)}, u32[]{:S(2)}, u32[]{:S(2)}) %collective-permute-start.1) | collective-permute-done | bytes 262176 | tf_op jit(solution)/shard_map/ppermute | solution.py:18
  29.9 6.6 %copy.43 = bf16[2,256,9,512]{1,3,2,0:T(8,128)(2,1)} copy(bf16[2,256,9,512]{3,1,0,2:T(8,128)(2,1)} %fusion.64) | data formatting | bytes 9437184 | tf_op jit(solution)/shard_map/stack | solution.py:39
  36.6 28.3 %all-gather.4.cloned.1.call-done = bf16[3,3,512,512]{3,2,1,0:T(8,128)(2,1)} async-done(((bf16[3,3,32,512]{3,2,1,0:T(8,128)(2,1)}), bf16[3,3,512,512]{3,2,1,0:T(8,128)(2,1)}) %all-gather.4.cloned.1.call-update) | async-done | bytes 4718608 | tf_op jit(solution)/shard_map/all_gather | solution.py:35
  64.9 6.7 %fusion.34 = (bf16[2,256,512]{2,1,0:T(8,128)(2,1)S(1)}, bf16[2,256,512]{2,1,0:T(8,128)(2,1)S(1)}) fusion(bf16[2,256,4608]{1,2,0:T(8,128)(2,1)} %bitcast.203, bf16[4608,512,1]{1,0,2:T(8,128)(2,1)} %bitcast.219, bf16[2,256,512]{2,1,0:T(8,128)(2,1)S(1)} %copy-done.2), kind=kOutput, calls=%fused_computation.64 | convolution fusion | flops 2419326976 | bytes 11010048 | tf_op jit(solution)/shard_map/dot_general | solution.py:48
  71.6 2.3 collective-permute-start.2
  74.0 2.0 collective-permute-start.3
  76.0 4.7 %collective-permute-done.2 = bf16[1,256,512]{2,1,0:T(8,128)(2,1)S(1)} collective-permute-done((bf16[1,256,512]{2,1,0:T(8,128)(2,1)S(1)}, bf16[1,256,512]{2,1,0:T(8,128)(2,1)S(1)}, u32[]{:S(2)}, u32[]{:S(2)}) %collective-permute-start.2) | collective-permute-done | bytes 262176 | tf_op jit(solution)/shard_map/ppermute | solution.py:17
  80.7 4.0 %collective-permute-done.3 = bf16[1,256,512]{2,1,0:T(8,128)(2,1)S(1)} collective-permute-done((bf16[1,256,512]{2,1,0:T(8,128)(2,1)S(1)}, bf16[1,256,512]{2,1,0:T(8,128)(2,1)S(1)}, u32[]{:S(2)}, u32[]{:S(2)}) %collective-permute-start.3) | collective-permute-done | bytes 262176 | tf_op jit(solution)/shard_map/ppermute | solution.py:18
  93.2 6.7 %copy.45 = bf16[2,256,9,512]{1,3,2,0:T(8,128)(2,1)} copy(bf16[2,256,9,512]{3,1,0,2:T(8,128)(2,1)} %fusion.54) | data formatting | bytes 9437184 | tf_op jit(solution)/shard_map/stack | solution.py:39
  100.0 20.6 %all-gather.6.cloned.1.call-done = bf16[3,3,512,512]{3,2,1,0:T(8,128)(2,1)} async-done(((bf16[3,3,32,512]{3,2,1,0:T(8,128)(2,1)}), bf16[3,3,512,512]{3,2,1,0:T(8,128)(2,1)}) %all-gather.6.cloned.1.call-update) | async-done | bytes 4718608 | tf_op jit(solution)/shard_map/all_gather | solution.py:35
  120.5 6.5 %fusion.18 = (f32[2,256]{1,0:T(2,128)S(1)}, bf16[2,256,512]{2,1,0:T(8,128)(2,1)S(1)}) fusion(bf16[2,256,4608]{1,2,0:T(8,128)(2,1)} %bitcast.202, bf16[4608,512,1]{1,0,2:T(8,128)(2,1)} %bitcast.218, bf16[2,256,512]{2,1,0:T(8,128)(2,1)S(1)} %get-tuple-element.7), kind=kOutput, calls=%fused_computation.48 | convolution fusion | flops 2417491456 | bytes 10487808 | tf_op jit(solution)/shard_map/dot_general | solution.py:48
  129.0 3.8 %all-to-all-start.1 = ((bf16[2,16,16,512]{3,1,0,2:T(8,128)(2,1)}), bf16[2,16,16,512]{3,1,0,2:T(8,128)(2,1)S(1)}, u32[]{:S(2)}, u32[]{:S(2)}) async-start(bf16[2,16,16,512]{3,1,0,2:T(8,128)(2,1)} %copy.48), calls=%async_computation.1 | async-start | bytes 1048576 | tf_op jit(solution)/shard_map/all_to_all | solution.py:89
  135.3 11.6 %all-to-all-done.1 = bf16[2,16,16,512]{3,1,0,2:T(8,128)(2,1)S(1)} async-done(((bf16[2,16,16,512]{3,1,0,2:T(8,128)(2,1)}), bf16[2,16,16,512]{3,1,0,2:T(8,128)(2,1)S(1)}, u32[]{:S(2)}, u32[]{:S(2)}) %all-to-all-start.1) | async-done | bytes 524320 | tf_op jit(solution)/shard_map/all_to_all | solution.py:89
  146.9 4.3 %all-to-all-start.2 = ((bf16[2,16,16,512]{3,1,0,2:T(8,128)(2,1)}), bf16[2,16,16,512]{3,1,0,2:T(8,128)(2,1)}, u32[]{:S(2)}, u32[]{:S(2)}) async-start(bf16[2,16,16,512]{3,1,0,2:T(8,128)(2,1)} %copy.49), calls=%async_computation.2 | async-start | bytes 1048576 | tf_op jit(solution)/shard_map/all_to_all | solution.py:90
  153.8 11.7 %all-to-all-done.2 = bf16[2,16,16,512]{3,1,0,2:T(8,128)(2,1)} async-done(((bf16[2,16,16,512]{3,1,0,2:T(8,128)(2,1)}), bf16[2,16,16,512]{3,1,0,2:T(8,128)(2,1)}, u32[]{:S(2)}, u32[]{:S(2)}) %all-to-all-start.2) | async-done | bytes 524320 | tf_op jit(solution)/shard_map/all_to_all | solution.py:90
  165.4 4.3 %all-to-all-start = ((bf16[2,16,16,512]{3,1,0,2:T(8,128)(2,1)}), bf16[2,16,16,512]{3,1,0,2:T(8,128)(2,1)}, u32[]{:S(2)}, u32[]{:S(2)}) async-start(bf16[2,16,16,512]{3,1,0,2:T(8,128)(2,1)} %copy.47), calls=%async_computation | async-start | bytes 1048576 | tf_op jit(solution)/shard_map/all_to_all | solution.py:91
  172.1 2.4 reshape.112
  174.5 9.5 %all-to-all-done = bf16[2,16,16,512]{3,1,0,2:T(8,128)(2,1)} async-done(((bf16[2,16,16,512]{3,1,0,2:T(8,128)(2,1)}), bf16[2,16,16,512]{3,1,0,2:T(8,128)(2,1)}, u32[]{:S(2)}, u32[]{:S(2)}) %all-to-all-start) | async-done | bytes 524320 | tf_op jit(solution)/shard_map/all_to_all | solution.py:91
  184.0 2.4 reshape.108
  186.4 14.5 %multiply_reduce_fusion = (f32[2,8,16,16]{3,2,1,0:T(8,128)S(1)}, f32[2,8,16,16,16,16]{3,5,4,2,1,0:T(8,128)}) fusion(bf16[16,2,16,8,64,1]{4,3,2,1,0,5:T(8,128)(2,1)} %bitcast.201, bf16[16,2,16,8,64,1]{4,3,2,1,0,5:T(8,128)(2,1)S(1)} %bitcast.200), kind=kOutput, calls=%fused_computation.2 | convolution fusion | flops 136310784 | bytes 5259264 | tf_op jit(solution)/shard_map/arbhd,erfhd->rhabef/dot_general | solution.py:97
  200.8 14.6 %fusion = f32[2,8,16,16]{3,2,1,0:T(8,128)S(1)} fusion(f32[2,8,16,16,16,16]{3,5,4,2,1,0:T(8,128)} %get-tuple-element.11, f32[2,8,16,16]{3,2,1,0:T(8,128)S(1)} %get-tuple-element.10), kind=kLoop, calls=%fused_computation.3 | loop fusion | flops 3141632 | bytes 4227072 | tf_op jit(solution)/shard_map/reduce_sum | solution.py:31
  215.5 15.3 %fusion.13 = bf16[16,2,16,8,64]{4,2,0,3,1:T(8,128)(2,1)} fusion(f32[2,8,16,16,16,16]{3,5,4,2,1,0:T(8,128)} %get-tuple-element.11, f32[2,8,16,16]{3,2,1,0:T(8,128)S(1)} %fusion, f32[2,8,16,16]{3,2,1,0:T(8,128)S(1)} %get-tuple-element.10, bf16[16,2,16,8,64,1]{4,3,2,1,0,5:T(8,128)(2,1)S(1)} %bitcast.210), kind=kOutput, calls=%fused_computation.35 | convolution fusion | flops 138674176 | bytes 5275648 | tf_op jit(solution)/shard_map/rhabef,erfhd->arbhd/dot_general | solution.py:105
  230.8 2.4 copy.54
  234.7 18.5 %all_to_all.75 = bf16[32,16,1,512]{3,1,2,0:T(8,128)(2,1)S(1)} all-to-all(bf16[32,16,1,512]{3,1,2,0:T(8,128)(2,1)} %bitcast.206), channel_id=1, replica_groups=mesh['parts'=2,'row'=16] {'row'}, dimensions={0} | all-to-all | bytes 1048576 | tf_op jit(solution)/shard_map/all_to_all | solution.py:112
  253.5 1.7 fusion.20
  255.4 5.2 %fusion.11 = f32[512,512]{1,0:T(8,128)} fusion(bf16[2048,512]{1,0:T(8,128)(2,1)S(1)} %copy-done, bf16[512,512]{1,0:T(8,128)(2,1)S(1)} %bitcast.214, bf16[512,2048]{1,0:T(8,128)(2,1)} %param.17), kind=kOutput, calls=%fused_computation.28 | convolution fusion | flops 2156920832 | bytes 5767168 | tf_op jit(solution)/shard_map/dot_general | solution.py:123
  263.2 14.2 %all_to_all.76 = bf16[2,16,10,512]{3,0,2,1:T(2,128)(2,1)S(1)} all-to-all(bf16[2,16,10,512]{3,0,2,1:T(2,128)(2,1)S(1)} %pad_maximum_fusion.4), channel_id=1, replica_groups=mesh['parts'=2,'row'=16] {'row'}, dimensions={1} | all-to-all | bytes 655360 | tf_op jit(solution)/shard_map/all_to_all | solution.py:137
  279.2 6.4 %copy.63 = bf16[32,16,9,512]{3,2,1,0:T(8,128)(2,1)} copy(bf16[32,16,9,512]{3,0,1,2:T(8,128)(2,1)S(1)} %fusion.50) | data formatting | bytes 9437184 | tf_op jit(solution)/shard_map/stack | solution.py:39
  285.6 10.2 %dot_general.54 = bf16[32,16,4608]{2,1,0:T(8,128)(2,1)} reshape(bf16[32,16,9,512]{3,2,1,0:T(8,128)(2,1)} %copy.63) | data formatting | bytes 9437184 | tf_op jit(solution)/shard_map/dot_general | solution.py:48
  295.8 7.2 %convolution_convert_fusion = bf16[32,16,512]{2,1,0:T(8,128)(2,1)} fusion(bf16[32,16,4608]{2,1,0:T(8,128)(2,1)} %dot_general.54, bf16[4608,512,1]{1,0,2:T(8,128)(2,1)} %bitcast.217), kind=kOutput, calls=%fused_computation.38 | convolution fusion | flops 2416181248 | bytes 9961472 | tf_op jit(solution)/shard_map/dot_general | solution.py:48
  (84 shorter events, 36.6 us)
Async XLA Ops:
  7.2 248.2 %copy-start = (bf16[2048,512]{1,0:T(8,128)(2,1)S(1)}, bf16[2048,512]{1,0:T(8,128)(2,1)}, u32[]{:S(2)}) copy-start(bf16[2048,512]{1,0:T(8,128)(2,1)} %param.18) | copy-start | bytes 6291460
  7.2 18.1 %copy-start.2 = (bf16[2,256,512]{2,1,0:T(8,128)(2,1)S(1)}, bf16[2,256,512]{2,1,0:T(8,128)(2,1)}, u32[]{:S(2)}) copy-start(bf16[2,256,512]{2,1,0:T(8,128)(2,1)} %param.10) | copy-start | bytes 1572868
  7.2 57.7 %all-gather.4.cloned.1.call-start = ((), (), s32[]{:S(2)}) async-start(), calls=%async_computation.5 | async-start | bytes 5013504 | tf_op jit(solution)/shard_map/all_gather | solution.py:35
  7.9 112.6 %all-gather.6.cloned.1.call-start = ((), (), s32[]{:S(2)}) async-start(), calls=%async_computation.6 | async-start | bytes 5013504 | tf_op jit(solution)/shard_map/all_gather | solution.py:35
  10.1 7.0 %collective-permute-start = (bf16[1,256,512]{2,1,0:T(8,128)(2,1)S(1)}, bf16[1,256,512]{2,1,0:T(8,128)(2,1)S(1)}, u32[]{:S(2)}, u32[]{:S(2)}) collective-permute-start(bf16[1,256,512]{2,1,0:T(8,128)(2,1)S(1)} %get-tuple-element.4), channel_id=1, source_target_pairs={{0,1},{1,2},{2,3},{3,4},{4,5},{5,6},{6,7},{7,8},{8,9},{9,10},{10,1... | collective-permute-start | bytes 786440 | tf_op jit(solution)/shard_map/ppermute | solution.py:17
  13.8 7.7 %collective-permute-start.1 = (bf16[1,256,512]{2,1,0:T(8,128)(2,1)S(1)}, bf16[1,256,512]{2,1,0:T(8,128)(2,1)S(1)}, u32[]{:S(2)}, u32[]{:S(2)}) collective-permute-start(bf16[1,256,512]{2,1,0:T(8,128)(2,1)S(1)} %get-tuple-element.5), channel_id=1, source_target_pairs={{1,0},{2,1},{3,2},{4,3},{5,4},{6,5},{7,6},{8,7},{9,8},{10,9},{11,1... | collective-permute-start | bytes 786440 | tf_op jit(solution)/shard_map/ppermute | solution.py:18
  71.6 9.1 %collective-permute-start.2 = (bf16[1,256,512]{2,1,0:T(8,128)(2,1)S(1)}, bf16[1,256,512]{2,1,0:T(8,128)(2,1)S(1)}, u32[]{:S(2)}, u32[]{:S(2)}) collective-permute-start(bf16[1,256,512]{2,1,0:T(8,128)(2,1)S(1)} %get-tuple-element.2), channel_id=1, source_target_pairs={{0,1},{1,2},{2,3},{3,4},{4,5},{5,6},{6,7},{7,8},{8,9},{9,10},{10,1... | collective-permute-start | bytes 786440 | tf_op jit(solution)/shard_map/ppermute | solution.py:17
  74.0 10.8 %collective-permute-start.3 = (bf16[1,256,512]{2,1,0:T(8,128)(2,1)S(1)}, bf16[1,256,512]{2,1,0:T(8,128)(2,1)S(1)}, u32[]{:S(2)}, u32[]{:S(2)}) collective-permute-start(bf16[1,256,512]{2,1,0:T(8,128)(2,1)S(1)} %get-tuple-element.3), channel_id=1, source_target_pairs={{1,0},{2,1},{3,2},{4,3},{5,4},{6,5},{7,6},{8,7},{9,8},{10,9},{11,1... | collective-permute-start | bytes 786440 | tf_op jit(solution)/shard_map/ppermute | solution.py:18
  120.5 6.7 %copy-start.5 = (bf16[512,512]{1,0:T(8,128)(2,1)S(1)}, bf16[512,512]{1,0:T(8,128)(2,1)}, u32[]{:S(2)}) copy-start(bf16[512,512]{1,0:T(8,128)(2,1)} %param.13) | copy-start | bytes 1572868
  127.1 0.8 copy-start.6
  129.0 17.9 %all-to-all-start.1 = ((bf16[2,16,16,512]{3,1,0,2:T(8,128)(2,1)}), bf16[2,16,16,512]{3,1,0,2:T(8,128)(2,1)S(1)}, u32[]{:S(2)}, u32[]{:S(2)}) async-start(bf16[2,16,16,512]{3,1,0,2:T(8,128)(2,1)} %copy.48), calls=%async_computation.1 | async-start | bytes 1048576 | tf_op jit(solution)/shard_map/all_to_all | solution.py:89
  146.9 23.5 %copy-start.1 = (bf16[2,16,16,512]{3,1,0,2:T(8,128)(2,1)}, bf16[2,16,16,512]{3,1,0,2:T(8,128)(2,1)S(1)}, u32[]{:S(2)}) copy-start(bf16[2,16,16,512]{3,1,0,2:T(8,128)(2,1)S(1)} %all-to-all-done.1) | copy-start | bytes 1572868
  146.9 18.5 %all-to-all-start.2 = ((bf16[2,16,16,512]{3,1,0,2:T(8,128)(2,1)}), bf16[2,16,16,512]{3,1,0,2:T(8,128)(2,1)}, u32[]{:S(2)}, u32[]{:S(2)}) async-start(bf16[2,16,16,512]{3,1,0,2:T(8,128)(2,1)} %copy.49), calls=%async_computation.2 | async-start | bytes 1048576 | tf_op jit(solution)/shard_map/all_to_all | solution.py:90
  165.4 18.5 %all-to-all-start = ((bf16[2,16,16,512]{3,1,0,2:T(8,128)(2,1)}), bf16[2,16,16,512]{3,1,0,2:T(8,128)(2,1)}, u32[]{:S(2)}, u32[]{:S(2)}) async-start(bf16[2,16,16,512]{3,1,0,2:T(8,128)(2,1)} %copy.47), calls=%async_computation | async-start | bytes 1048576 | tf_op jit(solution)/shard_map/all_to_all | solution.py:91
  169.7 126.1 %all-gather.8.cloned.1.call-start = ((), (), s32[]{:S(2)}) async-start(), calls=%async_computation.7 | async-start | bytes 5013504 | tf_op jit(solution)/shard_map/all_gather | solution.py:35
  200.8 14.6 %copy-start.4 = (bf16[16,2,16,8,64]{4,3,2,1,0:T(8,128)(2,1)S(1)}, bf16[16,2,16,8,64]{4,3,2,1,0:T(8,128)(2,1)}, u32[]{:S(2)}) copy-start(bf16[16,2,16,8,64]{4,3,2,1,0:T(8,128)(2,1)} %reshape.108) | copy-start | bytes 1572868
  262.0 16.4 %copy-start.3 = (bf16[2,256,512]{2,1,0:T(8,128)(2,1)}, bf16[2,256,512]{2,1,0:T(8,128)(2,1)S(1)}, u32[]{:S(2)}) copy-start(bf16[2,256,512]{2,1,0:T(8,128)(2,1)S(1)} %fusion.22) | copy-start | bytes 1572868
Sparse Core Ops, SparseCore 0:
  10.2 54.6 all-gather.3
  67.1 53.3 all-gather.5
  172.7 53.9 all-gather.7
where the time goes:
time: 313 us; the launch traced here: 309 us
  waiting for transfers between devices  98 us (31%)
  matrix products  60.5 us (19%)
  local copies, waits for them, and re-layouts  57 us (18%)
  blocking collectives  32.7 us (10%)
  other arithmetic  24.5 us (8%)
  starting transfers between devices  22.6 us (7%)
  between operations  14.1 us (5%)
    all_gather x3, waiting for transfers between devices, whole_kernel(): return lax.all_gather(kernel_piece, 'row', axis=2, tiled=True)  48.9 us
    another operation x6, local copies, waits for them, and re-layouts, convolve(): jnp.stack([padded[shift_row:shift_row + out_rows, shift_col:shift_col + o...  21.8 us
    dot_general x3, matrix products, convolve(): jnp.dot(tap_stack.reshape(-1, 9 * in_chans), kernel.reshape(9 * in_chans,...  20.4 us
    all_to_all x1, blocking collectives, on_device(): lax.all_to_all(attended, 'row', split_axis=0, concat_axis=2, tiled=True)  18.5 us
    dot_general x1, matrix products, on_device(): jnp.einsum('rhabef,erfhd->arbhd', probs, value_win.reshape(window_shape),...  15.3 us
    reduce_sum x1, other arithmetic, softmax_round(): jnp.sum(lifted, axis=-1, keepdims=True)  14.6 us
    dot_general x1, matrix products, on_device(): jnp.einsum('arbhd,erfhd->rhabef', query_win.reshape(window_shape), key_wi...  14.5 us
    all_to_all x1, blocking collectives, on_device(): lax.all_to_all(outgoing, 'row', split_axis=1, concat_axis=0, tiled=True)  14.2 us
  transfers between devices with their start and end apart: 10, of which 9 were waited for; matrix products, arithmetic and copies ran while one was open for 41% of the time, Pallas kernels for 0%

commit v1 on v0

v1 whole, which is shorter than its diff:
```python
import functools

import jax
import jax.numpy as jnp
from jax import lax
from jax.experimental import pallas as pl
from jax.experimental.pallas import tpu as pltpu
from jax.sharding import PartitionSpec as P

HD = 64
GRID = 16
F32 = jnp.float32
BF16 = jnp.bfloat16


def gelu(values):
    return jax.nn.gelu(values.astype(F32)).astype(BF16)


def rms_round(values):
    meansq = jnp.mean(values * values, axis=-1, keepdims=True)
    return (values * lax.rsqrt(meansq + 1e-06)).astype(BF16)


def dot(a, b):
    return jnp.dot(a, b, preferred_element_type=F32)


def conv_body(rows, top_ref, mid_ref, bot_ref, k_ref, res_ref, o_ref, act_ref):
    @pl.when(pl.program_id(0) == 0)
    def _():
        act_ref[0] = gelu(top_ref[0])
        for i in range(rows):
            act_ref[i + 1] = gelu(mid_ref[i])
        act_ref[rows + 1] = gelu(bot_ref[0])

    cols = act_ref.shape[1]
    width = k_ref.shape[3]
    col = lax.broadcasted_iota(jnp.int32, (cols, width), 0)
    for i in range(rows):
        sums = []
        for v in range(3):
            s = dot(act_ref[i], k_ref[0, v])
            s = s + dot(act_ref[i + 1], k_ref[1, v])
            s = s + dot(act_ref[i + 2], k_ref[2, v])
            sums.append(s)
        left = jnp.where(col == 0, 0.0, pltpu.roll(sums[0], 1, 0))
        right = jnp.where(col == cols - 1, 0.0, pltpu.roll(sums[2], cols - 1, 0))
        total = sums[1] + left + right
        o_ref[i] = (res_ref[i].astype(F32) + total).astype(BF16)


def conv_block(top, mid, bot, kernel, residual):
    rows, cols, channels = mid.shape
    out_channels = kernel.shape[3]
    width = min(256, out_channels)
    whole = lambda n: pl.BlockSpec((n, cols, channels), lambda b: (0, 0, 0))
    part = pl.BlockSpec((rows, cols, width), lambda b: (0, 0, b))
    return pl.pallas_call(
        functools.partial(conv_body, rows),
        grid=(out_channels // width,),
        in_specs=[
            whole(1),
            whole(rows),
            whole(1),
            pl.BlockSpec((3, 3, channels, width), lambda b: (0, 0, 0, b)),
            part,
        ],
        out_specs=part,
        out_shape=jax.ShapeDtypeStruct((rows, cols, out_channels), BF16),
        scratch_shapes=[pltpu.VMEM((rows + 2, cols, channels), BF16)],
        compiler_params=pltpu.CompilerParams(vmem_limit_bytes=48 << 20),
        name="conv_block",
        cost_estimate=pl.CostEstimate(
            flops=18 * rows * cols * channels * out_channels,
            bytes_accessed=18 * channels * out_channels,
            transcendentals=0,
        ),
    )(top, mid, bot, kernel, residual)


def window_body(x_ref, wq_ref, wk_ref, wv_ref, wo_ref, wi_ref, wd_ref, o_ref, att_ref):
    shape = x_ref.shape
    channels = shape[-1]
    cells = shape[0] * shape[2]
    x = x_ref[:, 0].reshape(cells, channels).astype(F32)
    normed = rms_round(x)
    queries = dot(normed, wq_ref[...]).astype(BF16)
    keys = dot(normed, wk_ref[...]).astype(BF16)
    values = dot(normed, wv_ref[...]).astype(BF16)
    pair = 2 * HD
    lane = lax.broadcasted_iota(jnp.int32, (cells, pair), 1)
    zero = jnp.zeros((cells, pair), BF16)
    for p in range(channels // pair):
        q = queries[:, p * pair : (p + 1) * pair]
        k = keys[:, p * pair : (p + 1) * pair]
        v = values[:, p * pair : (p + 1) * pair]
        out = None
        for half in range(2):
            own = (lane < HD) if half == 0 else (lane >= HD)
            scores = lax.dot_general(
                jnp.where(own, q, zero), k, (((1,), (1,)), ((), ())), preferred_element_type=F32
            ) * HD ** (-0.5)
            lifted = jnp.exp(scores - jnp.max(scores, axis=-1, keepdims=True))
            probs = (lifted * (1.0 / jnp.sum(lifted, axis=-1, keepdims=True))).astype(BF16)
            term = dot(probs, jnp.where(own, v, zero))
            out = term if out is None else out + term
        att_ref[:, p * pair : (p + 1) * pair] = out.astype(BF16)
    y3 = (x + dot(att_ref[...], wo_ref[...])).astype(BF16).astype(F32)
    hidden = gelu(dot(rms_round(y3), wi_ref[...]))
    result = (y3 + dot(hidden, wd_ref[...])).astype(BF16)
    o_ref[:, 0] = result.reshape(shape[0], shape[2], channels)


def window_block(x, *weights):
    grid_cells, bands, others, channels = x.shape
    part = pl.BlockSpec((grid_cells, 1, others, channels), lambda b: (0, b, 0, 0))
    whole = [pl.BlockSpec(w.shape, lambda b: (0, 0), pipeline_mode=pl.Buffered(1)) for w in weights]
    cells = grid_cells * others
    work = sum(w.size for w in weights)
    return pl.pallas_call(
        window_body,
        grid=(bands,),
        in_specs=[part] + whole,
        out_specs=part,
        out_shape=jax.ShapeDtypeStruct(x.shape, BF16),
        scratch_shapes=[pltpu.VMEM((cells, channels), BF16)],
        compiler_params=pltpu.CompilerParams(vmem_limit_bytes=48 << 20),
        name="window_block",
        cost_estimate=pl.CostEstimate(
            flops=2 * bands * cells * (work + 2 * cells * channels),
            bytes_accessed=2 * work,
            transcendentals=bands * cells * (cells * channels // HD),
        ),
    )(x, *weights)


def up_body(d_ref, k_ref, o_ref):
    _, rows, cols, channels = d_ref.shape
    width = k_ref.shape[3]
    sums = []
    for u in range(3):
        s = None
        for v in range(3):
            term = dot(d_ref[v].reshape(rows * cols, channels), k_ref[u, v])
            s = term if s is None else s + term
        sums.append(s.reshape(rows, cols, width))
    for i in range(rows):
        even = sums[1][i] + sums[2][i]
        if i > 0:
            even = even + sums[0][i - 1]
        odd = sums[0][i] + sums[1][i]
        if i < rows - 1:
            odd = odd + sums[2][i + 1]
        o_ref[2 * i] = even.astype(BF16)
        o_ref[2 * i + 1] = odd.astype(BF16)


def up_block(doubled, kernel):
    _, rows, cols, channels = doubled.shape
    out_channels = kernel.shape[3]
    width = min(256, out_channels)
    return pl.pallas_call(
        up_body,
        grid=(out_channels // width,),
        in_specs=[
            pl.BlockSpec(doubled.shape, lambda b: (0, 0, 0, 0)),
            pl.BlockSpec((3, 3, channels, width), lambda b: (0, 0, 0, b)),
        ],
        out_specs=pl.BlockSpec((2 * rows, cols, width), lambda b: (0, 0, b)),
        out_shape=jax.ShapeDtypeStruct((2 * rows, cols, out_channels), BF16),
        compiler_params=pltpu.CompilerParams(vmem_limit_bytes=48 << 20),
        name="up_block",
        cost_estimate=pl.CostEstimate(
            flops=18 * rows * cols * channels * out_channels,
            bytes_accessed=18 * channels * out_channels,
            transcendentals=0,
        ),
    )(doubled, kernel)


def whole_kernel(kernel_piece):
    return lax.all_gather(kernel_piece, "row", axis=2, tiled=True)


def edge_rows(value):
    size = lax.axis_size("row")
    up = [(i, i + 1) for i in range(size - 1)]
    down = [(j, i) for i, j in up]
    before = lax.ppermute(value[-1:], "row", up)
    after = lax.ppermute(value[:1], "row", down)
    return before, after


def convolve(padded, kernel, out_rows, out_cols):
    total = 0.0
    for u in range(3):
        for v in range(3):
            taps = padded[u : u + out_rows, v : v + out_cols]
            total = total + dot(taps.reshape(-1, taps.shape[2]), kernel[u, v])
    return total


def central_by_rows(latent_out, devices):
    grid_rows, grid_cols, channels = latent_out.shape
    central = latent_out[:, grid_cols // 4 : 3 * grid_cols // 4]
    central_cols = central.shape[1]
    slice_cols = central_cols // devices
    padded = jnp.pad(central, ((0, 0), (1, 1), (0, 0)))
    left = padded[:, :central_cols].reshape(grid_rows, devices, slice_cols, channels)
    first = padded[:, slice_cols::slice_cols]
    second = padded[:, slice_cols + 1 :: slice_cols]
    outgoing = jnp.concatenate([left, first[:, :, None], second[:, :, None]], axis=2)
    arrived = lax.all_to_all(outgoing, "row", split_axis=1, concat_axis=0, tiled=True)
    total_rows = arrived.shape[0]
    return arrived[total_rows // 4 : 3 * total_rows // 4, 0]


def central_by_windows(windows):
    grid_cells, bands, others, channels = windows.shape
    low, high = grid_cells // 4, 3 * grid_cells // 4
    mine = lax.axis_index("row")
    central = windows[low:high, :, others // 4 : 3 * others // 4]
    rows = (high - low) * bands
    central = central.reshape(rows, -1, channels).transpose(1, 0, 2)
    blank = jnp.zeros_like(central[:1])
    even = jnp.where(mine == grid_cells - 1, jnp.concatenate([blank, central[:-1]]), central)
    odd = jnp.where(mine == 0, jnp.concatenate([central[1:], blank]), central)
    outgoing = jnp.stack([even, odd], axis=1).reshape(-1, rows, channels)
    arrived = lax.all_to_all(outgoing, "row", split_axis=0, concat_axis=0, tiled=True)
    half = grid_cells // 2
    if_even = jnp.concatenate([arrived[-1:], arrived[: half + 1]])
    if_odd = jnp.concatenate([arrived[half - 1 :], arrived[:1]])
    return jnp.where(mine % 2 == 0, if_even, if_odd).transpose(1, 0, 2)


def on_device(
    latent, conv_first, conv_second, w_query, w_key, w_value, w_out, w_in, w_down, conv_up
):
    devices = lax.axis_size("row")
    grid_rows, grid_cols, channels = latent.shape
    current = latent
    for piece in (conv_first, conv_second):
        before, after = edge_rows(current)
        current = conv_block(before, current, after, whole_kernel(piece), current)
    up_kernel = whole_kernel(conv_up)

    step = devices // GRID
    groups = None
    if step > 1:
        groups = [[j + step * c for c in range(GRID)] for j in range(step)]
    exchange = functools.partial(
        lax.all_to_all,
        axis_name="row",
        split_axis=0,
        concat_axis=0,
        tiled=True,
        axis_index_groups=groups,
    )
    by_column = current.reshape(grid_rows, -1, GRID, channels).transpose(2, 0, 1, 3)
    windows = window_block(
        exchange(by_column), w_query, w_key, w_value, w_out, w_in, w_down
    )
    fast = step == 1 and grid_cols == GRID * GRID and channels % 128 == 0
    if fast:
        framed = central_by_windows(windows)
    latent_out = exchange(windows).transpose(1, 2, 0, 3).reshape(grid_rows, grid_cols, channels)
    if not fast:
        framed = central_by_rows(latent_out, devices)
    cols = framed.shape[1] - 2
    doubled = jnp.repeat(framed, 2, axis=1)[:, 1:-1]
    if fast:
        taps = jnp.stack([doubled[:, v : v + 2 * cols] for v in range(3)])
        return latent_out, up_block(taps, up_kernel)
    doubled = jnp.pad(jnp.repeat(doubled, 2, axis=0), ((1, 1), (0, 0), (0, 0)))
    total_rows = doubled.shape[0] - 2
    upsampled = convolve(doubled, up_kernel, total_rows, 2 * cols).astype(BF16)
    return latent_out, upsampled.reshape(total_rows, 2 * cols, channels)


def solution(mesh):
    placed = (
        P(("parts", "row"), None, None),
        P(None, None, "row", None),
        P(None, None, "row", None),
        P(),
        P(),
        P(),
        P(),
        P(),
        P(),
        P(None, None, "row", None),
    )
    return jax.shard_map(
        on_device,
        mesh=mesh,
        in_specs=placed,
        out_specs=(P(("parts", "row"), None, None), P("parts", "row", None)),
        check_vma=False,
    )
```

time: 313 us -> 214 us (0.68)
  matrix products: 60.5 us -> 0 us
  local copies, waits for them, and re-layouts: 57 us -> 12.2 us
  waiting for transfers between devices: 98 us -> 138 us
  blocking collectives: 32.7 us -> 0 us
  other arithmetic: 24.5 us -> 0.9 us
  Pallas kernels: 0 us -> 23.4 us
    dot_general x10 -> x0, matrix products: 60.5 us -> none  [the longest x3 20.4 us: convolve(): jnp.dot(tap_stack.reshape(-1, 9 * in_chans), kernel.reshape(9 * in_chans,...]
    all_gather x3, waiting for transfers between devices: 48.9 us -> 86.5 us  [whole_kernel(): return lax.all_gather(kernel_piece, 'row', axis=2, tiled=True)]
    all_to_all x2 -> x0, blocking collectives: 32.7 us -> none  [the longest x1 18.5 us: on_device(): lax.all_to_all(attended, 'row', split_axis=0, concat_axis=2, tiled=True)]
    pallas_call x0 -> x4, Pallas kernels: none -> 23.4 us  [the longest x2 10.5 us: conv_block(): pl.pallas_call(functools.partial(conv_body, rows), grid=(out_channels //...]
    another operation x6 -> x1, local copies, waits for them, and re-layouts: 21.8 us -> 0.29 us  [on_device(): taps = jnp.stack([doubled[:, v:v + 2 * cols] for v in range(3)])]
    reduce_sum x1 -> x0, other arithmetic: 14.6 us -> none  [softmax_round(): jnp.sum(lifted, axis=-1, keepdims=True)]
    all_to_all x3, waiting for transfers between devices: 32.7 us -> 43.4 us  [the longest x1 22.2 us: on_device(): exchange(by_column)]
    reshape x10 -> x2, local copies, waits for them, and re-layouts: 11.6 us -> 1.13 us  [the longest x1 1.09 us: on_device(): current.reshape(grid_rows, -1, GRID, channels).transpose(2, 0, 1, 3)]
  transfers between devices with their start and end apart: 10 -> 10, of which waited for: 9 -> 7; matrix products, arithmetic and copies ran while one was open for 41% -> 3% of each run, Pallas kernels for 0% -> 11%
where the time goes in v1:
time: 214 us; the launch traced here: 212 us
  waiting for transfers between devices  138 us (64%)
  starting transfers between devices  23.7 us (11%)
  Pallas kernels  23.4 us (11%)
  between operations  13.9 us (6%)
  local copies, waits for them, and re-layouts  12.2 us (6%)
    all_gather x3, waiting for transfers between devices, whole_kernel(): return lax.all_gather(kernel_piece, 'row', axis=2, tiled=True)  86.5 us
    all_to_all x1, waiting for transfers between devices, on_device(): exchange(by_column)  22.2 us
    all_to_all x1, waiting for transfers between devices, central_by_windows(): lax.all_to_all(outgoing, 'row', split_axis=0, concat_axis=0, tiled=True)  12.8 us
    pallas_call x2, Pallas kernels, conv_block(): pl.pallas_call(functools.partial(conv_body, rows), grid=(out_channels //...  10.5 us
    pallas_call x1, Pallas kernels, window_block(): pl.pallas_call(window_body, grid=(bands,), in_specs=[part] + whole, out_s...  10.4 us
    all_to_all x1, waiting for transfers between devices, on_device(): exchange(windows).transpose(1, 2, 0, 3)  8.39 us
    unnamed x15, local copies, waits for them, and re-layouts  6.66 us
    ppermute x2, starting transfers between devices, edge_rows(): before = lax.ppermute(value[-1:], 'row', up)  6.02 us
  transfers between devices with their start and end apart: 10, of which 7 were waited for; matrix products, arithmetic and copies ran while one was open for 3% of the time, Pallas kernels for 11%

profile of v1, /device:TPU:9, one launch (start us, length us, event | category | flops | bytes accessed | tf_op | source)
XLA Modules:
  0.0 212.4 jit_solution(13446646226884530171)
XLA Ops:
  7.2 0.7 all-gather.4.cloned.1.call-update
  7.9 0.7 all-gather.6.cloned.1.call-update
  8.7 0.7 all-gather.8.cloned.1.call-update
  9.4 1.1 fusion.2
  10.5 3.7 %collective-permute-start = (bf16[1,256,512]{2,1,0:T(8,128)(2,1)S(1)}, bf16[1,256,512]{2,1,0:T(8,128)(2,1)S(1)}, u32[]{:S(2)}, u32[]{:S(2)}) collective-permute-start(bf16[1,256,512]{2,1,0:T(8,128)(2,1)S(1)} %get-tuple-element.5), channel_id=1, source_target_pairs={{0,1},{1,2},{2,3},{3,4},{4,5},{5,6},{6,7},{7,8},{8,9},{9,10},{10,1... | collective-permute-start | bytes 786440 | tf_op jit(solution)/shard_map/ppermute | solution.py:190
  14.2 1.9 collective-permute-start.1
  16.1 1.4 collective-permute-done.top_ref
  17.5 4.8 %collective-permute-done.1.bot_ref = bf16[1,256,512]{2,1,0:T(8,128)(2,1)S(1)} collective-permute-done((bf16[1,256,512]{2,1,0:T(8,128)(2,1)S(1)}, bf16[1,256,512]{2,1,0:T(8,128)(2,1)S(1)}, u32[]{:S(2)}, u32[]{:S(2)}) %collective-permute-start.1) | collective-permute-done | bytes 262176 | tf_op jit(solution)/shard_map/ppermute | solution.py:191
  22.3 42.9 %all-gather.4.cloned.1.call-done.k_ref = bf16[3,3,512,512]{3,2,1,0:T(8,128)(2,1)} async-done(((bf16[3,3,32,512]{3,2,1,0:T(8,128)(2,1)}), bf16[3,3,512,512]{3,2,1,0:T(8,128)(2,1)}) %all-gather.4.cloned.1.call-update) | async-done | bytes 4718608 | tf_op jit(solution)/shard_map/all_gather | solution.py:183
  65.2 1.0 copy-done.1
  66.2 5.2 %conv_block.2.mid_ref.res_ref = bf16[2,256,512]{2,1,0:T(8,128)(2,1)S(1)} custom-call(bf16[1,256,512]{2,1,0:T(8,128)(2,1)S(1)} %collective-permute-done.top_ref, bf16[2,256,512]{2,1,0:T(8,128)(2,1)S(1)} %copy-done.1, bf16[1,256,512]{2,1,0:T(8,128)(2,1)S(1)} %collective-permute-done.1.bot_ref, bf16[3,3,512,512]{3,2,1,0:T(8,128)(2,1)} %all-gather.4.cloned.1.call-done.k_ref, ...), custom_call_target="tpu_custom_call" | custom-call | flops 2415919104 | bytes 4718592 | tf_op jit(solution)/shard_map/conv_block/pallas_call | solution.py:59
  71.5 0.8 fusion.1
  72.3 2.3 %collective-permute-start.2 = (bf16[1,256,512]{2,1,0:T(8,128)(2,1)}, bf16[1,256,512]{2,1,0:T(8,128)(2,1)S(1)}, u32[]{:S(2)}, u32[]{:S(2)}) collective-permute-start(bf16[1,256,512]{2,1,0:T(8,128)(2,1)} %get-tuple-element.3), channel_id=1, source_target_pairs={{0,1},{1,2},{2,3},{3,4},{4,5},{5,6},{6,7},{7,8},{8,9},{9,10},{10,1... | collective-permute-start | bytes 786440 | tf_op jit(solution)/shard_map/ppermute | solution.py:190
  74.6 2.3 %collective-permute-start.3 = (bf16[1,256,512]{2,1,0:T(8,128)(2,1)}, bf16[1,256,512]{2,1,0:T(8,128)(2,1)}, u32[]{:S(2)}, u32[]{:S(2)}) collective-permute-start(bf16[1,256,512]{2,1,0:T(8,128)(2,1)} %get-tuple-element.2), channel_id=1, source_target_pairs={{1,0},{2,1},{3,2},{4,3},{5,4},{6,5},{7,6},{8,7},{9,8},{10,9},{11,1... | collective-permute-start | bytes 786440 | tf_op jit(solution)/shard_map/ppermute | solution.py:191
  76.9 43.5 %all-gather.6.cloned.1.call-done.k_ref = bf16[3,3,512,512]{3,2,1,0:T(8,128)(2,1)} async-done(((bf16[3,3,32,512]{3,2,1,0:T(8,128)(2,1)}), bf16[3,3,512,512]{3,2,1,0:T(8,128)(2,1)}) %all-gather.6.cloned.1.call-update) | async-done | bytes 4718608 | tf_op jit(solution)/shard_map/all_gather | solution.py:183
  120.5 5.2 %conv_block.3 = bf16[2,256,512]{2,1,0:T(8,128)(2,1)S(1)} custom-call(bf16[1,256,512]{2,1,0:T(8,128)(2,1)S(1)} %collective-permute-done.2.top_ref, bf16[2,256,512]{2,1,0:T(8,128)(2,1)S(1)} %conv_block.2.mid_ref.res_ref, bf16[1,256,512]{2,1,0:T(8,128)(2,1)} %collective-permute-done.3.bot_ref, bf16[3,3,512,512]{3,2,1,0:T(8,128)(2,1)} %all-gather.6.cloned.1.call-done.k_ref, ...), custom_call_target="tpu_custom_call" | custom-call | flops 2415919104 | bytes 4718592 | tf_op jit(solution)/shard_map/conv_block/pallas_call | solution.py:59
  125.7 1.1 copy.31
  126.8 3.8 %all-to-all-start = ((bf16[16,2,16,512]{3,2,1,0:T(8,128)(2,1)}), bf16[16,2,16,512]{3,2,1,0:T(8,128)(2,1)S(1)}, u32[]{:S(2)}, u32[]{:S(2)}) async-start(bf16[16,2,16,512]{3,2,1,0:T(8,128)(2,1)} %bitcast.34), calls=%async_computation | async-start | bytes 1048576 | tf_op jit(solution)/shard_map/all_to_all | solution.py:262
  130.6 22.2 %all-to-all-done.x_ref = bf16[16,2,16,512]{3,2,1,0:T(8,128)(2,1)S(1)} async-done(((bf16[16,2,16,512]{3,2,1,0:T(8,128)(2,1)}), bf16[16,2,16,512]{3,2,1,0:T(8,128)(2,1)S(1)}, u32[]{:S(2)}, u32[]{:S(2)}) %all-to-all-start) | async-done | bytes 524320 | tf_op jit(solution)/shard_map/all_to_all | solution.py:262
  152.8 1.0 copy-done.4
  153.9 1.0 copy-done.5
  154.9 1.0 copy-done.6
  156.0 10.4 %window_block.1 = bf16[16,2,16,512]{3,2,1,0:T(8,128)(2,1)} custom-call(bf16[16,2,16,512]{3,2,1,0:T(8,128)(2,1)S(1)} %all-to-all-done.x_ref, bf16[512,512]{1,0:T(8,128)(2,1)S(1)} %copy-done.3, bf16[512,512]{1,0:T(8,128)(2,1)S(1)} %copy-done.4, bf16[512,512]{1,0:T(8,128)(2,1)S(1)} %copy-done.5, bf16[512,512]{1,0:T(8,128)(2,1)S(1)} %copy-done.6, ...), custom_call_target="tpu_custom_call" | custom-call | flops 3489660928 | bytes 6291456 | tf_op jit(solution)/shard_map/window_block/pallas_call | solution.py:121
  166.4 1.0 slice.62
  167.5 0.7 pad_maximum_fusion.1
  168.2 4.4 %all-to-all-start.2 = ((bf16[16,16,512]{2,1,0:T(8,128)(2,1)}), bf16[16,16,512]{2,1,0:T(8,128)(2,1)S(1)}, u32[]{:S(2)}, u32[]{:S(2)}) async-start(bf16[16,16,512]{2,1,0:T(8,128)(2,1)} %bitcast.9), calls=%async_computation.2 | async-start | bytes 524288 | tf_op jit(solution)/shard_map/all_to_all | solution.py:230
  172.6 12.8 %all-to-all-done.2 = bf16[16,16,512]{2,1,0:T(8,128)(2,1)S(1)} async-done(((bf16[16,16,512]{2,1,0:T(8,128)(2,1)}), bf16[16,16,512]{2,1,0:T(8,128)(2,1)S(1)}, u32[]{:S(2)}, u32[]{:S(2)}) %all-to-all-start.2) | async-done | bytes 262176 | tf_op jit(solution)/shard_map/all_to_all | solution.py:230
  185.4 5.3 %all-to-all-start.1 = ((bf16[16,2,16,512]{3,2,1,0:T(8,128)(2,1)}), bf16[16,2,16,512]{3,2,1,0:T(8,128)(2,1)S(1)}, u32[]{:S(2)}, u32[]{:S(2)}) async-start(bf16[16,2,16,512]{3,2,1,0:T(8,128)(2,1)} %window_block.1), calls=%async_computation.1 | async-start | bytes 1048576 | tf_op jit(solution)/shard_map/all_to_all | solution.py:267
  191.4 2.3 %copy-done = bf16[3,3,512,512]{3,2,1,0:T(8,128)(2,1)S(1)} copy-done((bf16[3,3,512,512]{3,2,1,0:T(8,128)(2,1)S(1)}, bf16[3,3,512,512]{3,2,1,0:T(8,128)(2,1)}, u32[]{:S(2)}) %copy-start) | copy-done | bytes 4718616
  193.8 2.6 %up_block.1 = bf16[32,16,512]{2,1,0:T(8,128)(2,1)} custom-call(bf16[3,16,16,512]{3,2,1,0:T(8,128)(2,1)S(1)} %pad_maximum_fusion.d_ref, bf16[3,3,512,512]{3,2,1,0:T(8,128)(2,1)S(1)} %copy-done), custom_call_target="tpu_custom_call" | custom-call | flops 1207959552 | bytes 4718592 | tf_op jit(solution)/shard_map/up_block/pallas_call | solution.py:163
  196.4 8.4 %all-to-all-done.1 = bf16[16,2,16,512]{3,2,1,0:T(8,128)(2,1)S(1)} async-done(((bf16[16,2,16,512]{3,2,1,0:T(8,128)(2,1)}), bf16[16,2,16,512]{3,2,1,0:T(8,128)(2,1)S(1)}, u32[]{:S(2)}, u32[]{:S(2)}) %all-to-all-start.1) | async-done | bytes 524320 | tf_op jit(solution)/shard_map/all_to_all | solution.py:267
  204.8 1.1 copy.13
  (26 shorter events, 1.0 us)
Async XLA Ops:
  7.2 58.0 %all-gather.4.cloned.1.call-start = ((), (), s32[]{:S(2)}) async-start(), calls=%async_computation.3 | async-start | bytes 5013504 | tf_op jit(solution)/shard_map/all_gather | solution.py:183
  7.9 112.6 %all-gather.6.cloned.1.call-start = ((), (), s32[]{:S(2)}) async-start(), calls=%async_computation.4 | async-start | bytes 5013504 | tf_op jit(solution)/shard_map/all_gather | solution.py:183
  8.6 182.8 %all-gather.8.cloned.1.call-start = ((), (), s32[]{:S(2)}) async-start(), calls=%async_computation.5 | async-start | bytes 5013504 | tf_op jit(solution)/shard_map/all_gather | solution.py:183
  10.5 7.0 %collective-permute-start = (bf16[1,256,512]{2,1,0:T(8,128)(2,1)S(1)}, bf16[1,256,512]{2,1,0:T(8,128)(2,1)S(1)}, u32[]{:S(2)}, u32[]{:S(2)}) collective-permute-start(bf16[1,256,512]{2,1,0:T(8,128)(2,1)S(1)} %get-tuple-element.5), channel_id=1, source_target_pairs={{0,1},{1,2},{2,3},{3,4},{4,5},{5,6},{6,7},{7,8},{8,9},{9,10},{10,1... | collective-permute-start | bytes 786440 | tf_op jit(solution)/shard_map/ppermute | solution.py:190
  14.2 8.1 %collective-permute-start.1 = (bf16[1,256,512]{2,1,0:T(8,128)(2,1)S(1)}, bf16[1,256,512]{2,1,0:T(8,128)(2,1)S(1)}, u32[]{:S(2)}, u32[]{:S(2)}) collective-permute-start(bf16[1,256,512]{2,1,0:T(8,128)(2,1)S(1)} %get-tuple-element.4), channel_id=1, source_target_pairs={{1,0},{2,1},{3,2},{4,3},{5,4},{6,5},{7,6},{8,7},{9,8},{10,9},{11,1... | collective-permute-start | bytes 786440 | tf_op jit(solution)/shard_map/ppermute | solution.py:191
  65.2 1.0 copy-start.1
  72.3 48.2 %collective-permute-start.2 = (bf16[1,256,512]{2,1,0:T(8,128)(2,1)}, bf16[1,256,512]{2,1,0:T(8,128)(2,1)S(1)}, u32[]{:S(2)}, u32[]{:S(2)}) collective-permute-start(bf16[1,256,512]{2,1,0:T(8,128)(2,1)} %get-tuple-element.3), channel_id=1, source_target_pairs={{0,1},{1,2},{2,3},{3,4},{4,5},{5,6},{6,7},{7,8},{8,9},{9,10},{10,1... | collective-permute-start | bytes 786440 | tf_op jit(solution)/shard_map/ppermute | solution.py:190
  74.6 78.2 %copy-start.2 = (bf16[512,2048]{1,0:T(8,128)(2,1)S(1)}, bf16[512,2048]{1,0:T(8,128)(2,1)}, u32[]{:S(2)}) copy-start(bf16[512,2048]{1,0:T(8,128)(2,1)} %wi_ref.1) | copy-start | bytes 6291460
  74.6 78.2 %copy-start.3 = (bf16[512,512]{1,0:T(8,128)(2,1)S(1)}, bf16[512,512]{1,0:T(8,128)(2,1)}, u32[]{:S(2)}) copy-start(bf16[512,512]{1,0:T(8,128)(2,1)} %wq_ref.1) | copy-start | bytes 1572868
  74.6 45.8 %collective-permute-start.3 = (bf16[1,256,512]{2,1,0:T(8,128)(2,1)}, bf16[1,256,512]{2,1,0:T(8,128)(2,1)}, u32[]{:S(2)}, u32[]{:S(2)}) collective-permute-start(bf16[1,256,512]{2,1,0:T(8,128)(2,1)} %get-tuple-element.2), channel_id=1, source_target_pairs={{1,0},{2,1},{3,2},{4,3},{5,4},{6,5},{7,6},{8,7},{9,8},{10,9},{11,1... | collective-permute-start | bytes 786440 | tf_op jit(solution)/shard_map/ppermute | solution.py:191
  126.8 26.0 %all-to-all-start = ((bf16[16,2,16,512]{3,2,1,0:T(8,128)(2,1)}), bf16[16,2,16,512]{3,2,1,0:T(8,128)(2,1)S(1)}, u32[]{:S(2)}, u32[]{:S(2)}) async-start(bf16[16,2,16,512]{3,2,1,0:T(8,128)(2,1)} %bitcast.34), calls=%async_computation | async-start | bytes 1048576 | tf_op jit(solution)/shard_map/all_to_all | solution.py:262
  152.8 1.0 copy-start.4
  153.9 1.0 copy-start.5
  154.9 1.0 copy-start.6
  168.2 17.2 %all-to-all-start.2 = ((bf16[16,16,512]{2,1,0:T(8,128)(2,1)}), bf16[16,16,512]{2,1,0:T(8,128)(2,1)S(1)}, u32[]{:S(2)}, u32[]{:S(2)}) async-start(bf16[16,16,512]{2,1,0:T(8,128)(2,1)} %bitcast.9), calls=%async_computation.2 | async-start | bytes 524288 | tf_op jit(solution)/shard_map/all_to_all | solution.py:230
  185.4 19.4 %all-to-all-start.1 = ((bf16[16,2,16,512]{3,2,1,0:T(8,128)(2,1)}), bf16[16,2,16,512]{3,2,1,0:T(8,128)(2,1)S(1)}, u32[]{:S(2)}, u32[]{:S(2)}) async-start(bf16[16,2,16,512]{3,2,1,0:T(8,128)(2,1)} %window_block.1), calls=%async_computation.1 | async-start | bytes 1048576 | tf_op jit(solution)/shard_map/all_to_all | solution.py:267
  191.4 2.3 %copy-start = (bf16[3,3,512,512]{3,2,1,0:T(8,128)(2,1)S(1)}, bf16[3,3,512,512]{3,2,1,0:T(8,128)(2,1)}, u32[]{:S(2)}) copy-start(bf16[3,3,512,512]{3,2,1,0:T(8,128)(2,1)} %all-gather.8.cloned.1.call-done.k_ref) | copy-start | bytes 14155780
Sparse Core Ops, SparseCore 0:
  10.2 54.9 all-gather.3
  67.4 53.0 all-gather.5
  122.7 64.3 all-gather.7

commit v2 on v1

--- a/solution.py
+++ b/solution.py
@@ -183,6 +183,235 @@
     return lax.all_gather(kernel_piece, "row", axis=2, tiled=True)
 
 
+def gather_body(count, nz, *refs):
+    pieces, wholes, owns = refs[:count], refs[count : 2 * count], refs[2 * count : 3 * count]
+    load_sem, keep_sem, zs, zr, ys, yr, xs, xr, cs, cr = refs[3 * count :]
+    index, part = lax.axis_index("row"), lax.axis_index("parts")
+    core, y, z = index % 2, (index // 2) % 2, index // 4
+    parity = part % 2
+    taps, rows, _ = pieces[0].shape
+    half = rows // 2
+    zero = nz - 1
+
+    def device(z_, y_, core_, part_):
+        return {"parts": part_, "row": (z_ * 2 + y_) * 2 + core_}
+
+    def place(ref, z_, y_, t):
+        base = ((z_ * 2 + y_) * 2 + core) * rows
+        size = rows
+        if t is not None:
+            base = base + ((parity + t) % 2) * half
+            size = half
+        return ref.at[:, pl.ds(pl.multiple_of(base, size), size)]
+
+    def source(m, d, t):
+        if d != 0:
+            return place(wholes[m], z - d, y, t)
+        if t is None:
+            return pieces[m]
+        return pieces[m].at[:, pl.ds(pl.multiple_of(((parity + t) % 2) * half, half), half)]
+
+    def remote(src, dst, send, recv, to):
+        return pltpu.make_async_remote_copy(
+            src_ref=src,
+            dst_ref=dst,
+            send_sem=send,
+            recv_sem=recv,
+            device_id=to,
+            device_id_type=pl.DeviceIdType.MESH,
+        )
+
+    def z_copy(m, d, t, way):
+        slot = d + way + zero
+        return remote(
+            source(m, d, t),
+            place(wholes[m], z - d, y, t),
+            zs.at[m, slot, t],
+            zr.at[m, slot, t],
+            device(z + way, y, core, part),
+        )
+
+    def z_arrival(m, d, t):
+        here = place(wholes[m], z - d, y, t)
+        way = 1 if d > 0 else -1
+        slot = d + zero
+        return remote(
+            here, here, zs.at[m, slot, t], zr.at[m, slot, t], device(z - way, y, core, part)
+        )
+
+    def y_copy(m, d):
+        slot = d + zero
+        return remote(
+            source(m, d, 0),
+            place(wholes[m], z - d, y, 0),
+            ys.at[m, slot],
+            yr.at[m, slot],
+            device(z, 1 - y, core, part),
+        )
+
+    def y_arrival(m, d):
+        here = place(wholes[m], z - d, 1 - y, 0)
+        slot = d + zero
+        return remote(here, here, ys.at[m, slot], yr.at[m, slot], device(z, 1 - y, core, part))
+
+    def x_copy(m, d):
+        here = place(wholes[m], z - d, 1 - y, 0)
+        slot = d + zero
+        to = device(z, y, core, part + 1 - 2 * parity)
+        return remote(here, here, xs.at[m, slot], xr.at[m, slot], to)
+
+    def x_arrival(m, d):
+        here = place(wholes[m], z - d, 1 - y, 1)
+        slot = d + zero
+        to = device(z, y, core, part + 1 - 2 * parity)
+        return remote(here, here, xs.at[m, slot], xr.at[m, slot], to)
+
+    def c_copy(m, column, d):
+        slot = d + zero
+        to = device(z, y, 1 - core, part)
+        if column == 0:
+            src, dst = source(m, d, None), place(wholes[m], z - d, y, None)
+        else:
+            src = place(wholes[m], z - d, 1 - y, None)
+            dst = src
+        return remote(src, dst, cs.at[m, column, slot], cr.at[m, column, slot], to)
+
+    def c_arrival(m, column, d):
+        slot = d + zero
+        y_ = y if column == 0 else 1 - y
+        base = ((z - d) * 2 + y_) * 2 + 1 - core
+        here = wholes[m].at[:, pl.ds(pl.multiple_of(base * rows, rows), rows)]
+        to = device(z, y, 1 - core, part)
+        return remote(here, here, cs.at[m, column, slot], cr.at[m, column, slot], to)
+
+    def when(condition, action):
+        if condition is None:
+            action()
+        else:
+            pl.when(condition)(action)
+
+    def valid(d):
+        if d == 0:
+            return None
+        return z >= d if d > 0 else z - d <= nz - 1
+
+    def ahead(way):
+        return z < nz - 1 if way > 0 else z > 0
+
+    def both(distance):
+        return (0,) if distance == 0 else (distance, -distance)
+
+    barrier = pltpu.get_barrier_semaphore()
+
+    def greet(to):
+        pl.semaphore_signal(
+            barrier, inc=1, device_id=to, device_id_type=pl.DeviceIdType.MESH
+        )
+
+    greet(device(z, 1 - y, core, part))
+    greet(device(z, y, 1 - core, part))
+    greet(device(z, y, core, part + 1 - 2 * parity))
+    for way in (1, -1):
+        when(ahead(way), functools.partial(greet, device(z + way, y, core, part)))
+    pl.semaphore_wait(barrier, 3 + jnp.minimum(z, 1) + jnp.minimum(nz - 1 - z, 1))
+
+    loads = [
+        pltpu.make_async_copy(pieces[m], owns[m], load_sem.at[m]) for m in range(count)
+    ]
+    keeps = [
+        pltpu.make_async_copy(owns[m], place(wholes[m], z, y, None), keep_sem.at[m])
+        for m in range(count)
+    ]
+    for m in range(count):
+        for t in range(2):
+            for way in (1, -1):
+                when(ahead(way), lambda: z_copy(m, 0, t, way).start())
+        y_copy(m, 0).start()
+        c_copy(m, 0, 0).start()
+        loads[m].start()
+    for m in range(count):
+        loads[m].wait()
+        keeps[m].start()
+
+    for distance in range(1, nz + 2):
+        for m in range(count):
+            if distance < nz:
+                for d in both(distance):
+                    way = 1 if d > 0 else -1
+
+                    def from_z():
+                        for t in range(2):
+                            z_arrival(m, d, t).wait_recv()
+                            if distance < nz - 1:
+                                when(ahead(way), lambda: z_copy(m, d, t, way).start())
+                            if t == 0:
+                                y_copy(m, d).start()
+                        c_copy(m, 0, d).start()
+
+                    when(valid(d), from_z)
+            if distance - 1 < nz:
+                for d in both(distance - 1):
+
+                    def from_y():
+                        y_arrival(m, d).wait_recv()
+                        x_copy(m, d).start()
+
+                    when(valid(d), from_y)
+            if 0 <= distance - 2 < nz:
+                for d in both(distance - 2):
+
+                    def from_x():
+                        x_arrival(m, d).wait_recv()
+                        c_copy(m, 1, d).start()
+
+                    when(valid(d), from_x)
+
+    for m in range(count):
+        keeps[m].wait()
+        for distance in range(nz):
+            for d in both(distance):
+
+                def finish():
+                    y_copy(m, d).wait_send()
+                    x_copy(m, d).wait_send()
+                    for column in range(2):
+                        c_copy(m, column, d).wait_send()
+                        c_arrival(m, column, d).wait_recv()
+                    for way in (1, -1):
+                        if d * way >= 0 and distance < nz - 1:
+                            for t in range(2):
+                                when(ahead(way), lambda: z_copy(m, d, t, way).wait_send())
+
+                when(valid(d), finish)
+
+
+def gather_kernels(pieces, collective_id):
+    devices = lax.axis_size("row")
+    nz = devices // 4
+    count = len(pieces)
+    flat = [p.reshape(-1, p.shape[2], p.shape[3]) for p in pieces]
+    taps, rows, out_channels = flat[0].shape
+    slots = 2 * nz - 1
+    dma = pltpu.SemaphoreType.DMA
+    anywhere = pl.BlockSpec(memory_space=pl.ANY)
+    outs = pl.pallas_call(
+        functools.partial(gather_body, count, nz),
+        in_specs=[anywhere] * count,
+        out_specs=[anywhere] * count,
+        out_shape=[jax.ShapeDtypeStruct((taps, rows * devices, out_channels), BF16)] * count,
+        scratch_shapes=[pltpu.VMEM((taps, rows, out_channels), BF16)] * count
+        + [dma((count,))] * 2
+        + [dma((count, slots, 2))] * 2
+        + [dma((count, slots))] * 4
+        + [dma((count, 2, slots))] * 2,
+        compiler_params=pltpu.CompilerParams(
+            collective_id=collective_id, has_side_effects=True, vmem_limit_bytes=16 << 20
+        ),
+        name="gather_kernels",
+    )(*flat)
+    return [o.reshape(3, 3, rows * devices, out_channels) for o in outs]
+
+
 def edge_rows(value):
     size = lax.axis_size("row")
     up = [(i, i + 1) for i in range(size - 1)]
@@ -227,11 +456,14 @@
     even = jnp.where(mine == grid_cells - 1, jnp.concatenate([blank, central[:-1]]), central)
     odd = jnp.where(mine == 0, jnp.concatenate([central[1:], blank]), central)
     outgoing = jnp.stack([even, odd], axis=1).reshape(-1, rows, channels)
-    arrived = lax.all_to_all(outgoing, "row", split_axis=0, concat_axis=0, tiled=True)
+    width = bands * others
+    both = jnp.concatenate([windows.reshape(grid_cells, width, channels), outgoing], axis=1)
+    both = lax.all_to_all(both, "row", split_axis=0, concat_axis=0, tiled=True)
+    returned, arrived = both[:, :width].reshape(windows.shape), both[:, width:]
     half = grid_cells // 2
     if_even = jnp.concatenate([arrived[-1:], arrived[: half + 1]])
     if_odd = jnp.concatenate([arrived[half - 1 :], arrived[:1]])
-    return jnp.where(mine % 2 == 0, if_even, if_odd).transpose(1, 0, 2)
+    return returned, jnp.where(mine % 2 == 0, if_even, if_odd).transpose(1, 0, 2)
 
 
 def on_device(
@@ -239,11 +471,16 @@
 ):
     devices = lax.axis_size("row")
     grid_rows, grid_cols, channels = latent.shape
+    paired = devices % 4 == 0 and lax.axis_size("parts") % 2 == 0
+    if paired and devices <= GRID and conv_first.shape[2] % 32 == 0:
+        kernels = gather_kernels([conv_first, conv_second], 0)
+    else:
+        kernels = [whole_kernel(conv_first), whole_kernel(conv_second)]
+    up_kernel = whole_kernel(conv_up)
     current = latent
-    for piece in (conv_first, conv_second):
+    for kernel in kernels:
         before, after = edge_rows(current)
-        current = conv_block(before, current, after, whole_kernel(piece), current)
-    up_kernel = whole_kernel(conv_up)
+        current = conv_block(before, current, after, kernel, current)
 
     step = devices // GRID
     groups = None
@@ -263,8 +500,10 @@
     )
     fast = step == 1 and grid_cols == GRID * GRID and channels % 128 == 0
     if fast:
-        framed = central_by_windows(windows)
-    latent_out = exchange(windows).transpose(1, 2, 0, 3).reshape(grid_rows, grid_cols, channels)
+        returned, framed = central_by_windows(windows)
+    else:
+        returned = exchange(windows)
+    latent_out = returned.transpose(1, 2, 0, 3).reshape(grid_rows, grid_cols, channels)
     if not fast:
         framed = central_by_rows(latent_out, devices)
     cols = framed.shape[1] - 2

time: 214 us -> 199 us (0.930)
  waiting for transfers between devices: 138 us -> 40.1 us
  Pallas kernels: 23.4 us -> 92.6 us
  starting transfers between devices: 23.7 us -> 33.6 us
  local copies, waits for them, and re-layouts: 12.2 us -> 16.8 us
    all_gather x3 -> x1, waiting for transfers between devices: 86.5 us -> 0.02 us  [whole_kernel(): return lax.all_gather(kernel_piece, 'row', axis=2, tiled=True)]
    pallas_call x0 -> x1, Pallas kernels: none -> 69.9 us  [gather_kernels(): pl.pallas_call(functools.partial(gather_body, count, nz), in_specs=[anywh...]
    all_to_all x1, starting transfers between devices: 3.78 us -> 18.4 us  [on_device(): exchange(by_column)]
    all_to_all x1, waiting for transfers between devices: 22.2 us -> 14.1 us  [on_device(): exchange(by_column)]
    unnamed x15 -> x23, local copies, waits for them, and re-layouts: 6.66 us -> 13 us
    all_to_all x2 -> x1, starting transfers between devices: 9.64 us -> 4.32 us  [central_by_windows(): both = lax.all_to_all(both, 'row', split_axis=0, concat_axis=0, tiled=True)]
    all_to_all x2 -> x1, waiting for transfers between devices: 21.2 us -> 19.6 us  [central_by_windows(): both = lax.all_to_all(both, 'row', split_axis=0, concat_axis=0, tiled=True)]
  transfers between devices with their start and end apart: 10 -> 7, of which waited for: 7 -> 4; matrix products, arithmetic and copies ran while one was open for 3% -> 3% of each run, Pallas kernels for 11% -> 45%
where the time goes in v2:
time: 199 us
  Pallas kernels  92.6 us (47%)
  waiting for transfers between devices  40.1 us (20%)
  starting transfers between devices  33.6 us (17%)
  local copies, waits for them, and re-layouts  16.8 us (8%)
  between operations  14.2 us (7%)
    pallas_call x1, Pallas kernels, gather_kernels(): pl.pallas_call(functools.partial(gather_body, count, nz), in_specs=[anywh...  69.9 us
    all_to_all x1, waiting for transfers between devices, central_by_windows(): both = lax.all_to_all(both, 'row', split_axis=0, concat_axis=0, tiled=True)  19.6 us
    all_to_all x1, starting transfers between devices, on_device(): exchange(by_column)  18.4 us
    all_to_all x1, waiting for transfers between devices, on_device(): exchange(by_column)  14.1 us
    unnamed x23, local copies, waits for them, and re-layouts  13 us
    pallas_call x2, Pallas kernels, conv_block(): pl.pallas_call(functools.partial(conv_body, rows), grid=(out_channels //...  10.5 us
    pallas_call x1, Pallas kernels, window_block(): pl.pallas_call(window_body, grid=(bands,), in_specs=[part] + whole, out_s...  9.52 us
    ppermute x2, starting transfers between devices, edge_rows(): before = lax.ppermute(value[-1:], 'row', up)  6.91 us
  transfers between devices with their start and end apart: 7, of which 4 were waited for; matrix products, arithmetic and copies ran while one was open for 3% of the time, Pallas kernels for 45%

profile of v2, /device:TPU:9, one launch (start us, length us, event | category | flops | bytes accessed | tf_op | source)
XLA Modules:
  0.0 198.5 jit_solution(11146834865936478259)
XLA Ops:
  7.2 0.7 all-gather.2.cloned.1.call-update
  7.9 1.1 fusion.4
  9.0 3.7 %collective-permute-start = (bf16[1,256,512]{2,1,0:T(8,128)(2,1)S(1)}, bf16[1,256,512]{2,1,0:T(8,128)(2,1)S(1)}, u32[]{:S(2)}, u32[]{:S(2)}) collective-permute-start(bf16[1,256,512]{2,1,0:T(8,128)(2,1)S(1)} %get-tuple-element.13), channel_id=1, source_target_pairs={{0,1},{1,2},{2,3},{3,4},{4,5},{5,6},{6,7},{7,8},{8,9},{9,10},{10,1... | collective-permute-start | bytes 786440 | tf_op jit(solution)/shard_map/ppermute | solution.py:419
  12.7 1.9 collective-permute-start.1
  14.6 1.0 copy-done.2
  15.6 1.0 copy-done.3
  16.5 69.9 %gather_kernels.1 = (bf16[9,512,512]{2,1,0:T(8,128)(2,1)S(1)}, bf16[9,512,512]{2,1,0:T(8,128)(2,1)S(1)}) custom-call(bf16[9,32,512]{2,1,0:T(8,128)(2,1)S(1)} %bitcast.40, bf16[9,32,512]{2,1,0:T(8,128)(2,1)S(1)} %bitcast.41), custom_call_target="tpu_custom_call" | custom-call | tf_op jit(solution)/shard_map/gather_kernels/pallas_call | solution.py:397
  86.5 2.2 %copy-done.4 = bf16[9,512,512]{2,1,0:T(8,128)(2,1)} copy-done((bf16[9,512,512]{2,1,0:T(8,128)(2,1)}, bf16[9,512,512]{2,1,0:T(8,128)(2,1)S(1)}, u32[]{:S(2)}) %copy-start.4) | copy-done | bytes 4718616
  88.7 2.2 %copy-done.5 = bf16[9,512,512]{2,1,0:T(8,128)(2,1)} copy-done((bf16[9,512,512]{2,1,0:T(8,128)(2,1)}, bf16[9,512,512]{2,1,0:T(8,128)(2,1)S(1)}, u32[]{:S(2)}) %copy-start.5) | copy-done | bytes 4718616
  90.9 1.0 copy-done.1
  92.0 5.2 %conv_block.2.mid_ref.res_ref = bf16[2,256,512]{2,1,0:T(8,128)(2,1)S(1)} custom-call(bf16[1,256,512]{2,1,0:T(8,128)(2,1)S(1)} %collective-permute-done.top_ref, bf16[2,256,512]{2,1,0:T(8,128)(2,1)S(1)} %copy-done.1, bf16[1,256,512]{2,1,0:T(8,128)(2,1)S(1)} %collective-permute-done.1.bot_ref, bf16[3,3,512,512]{3,2,1,0:T(8,128)(2,1)} %bitcast.43, ...), custom_call_target="tpu_custom_call" | custom-call | flops 2415919104 | bytes 4718592 | tf_op jit(solution)/shard_map/conv_block/pallas_call | solution.py:59
  97.2 3.2 %collective-permute-start.2 = (bf16[1,256,512]{2,1,0:T(8,128)(2,1)S(1)}, bf16[1,256,512]{2,1,0:T(8,128)(2,1)S(1)}, u32[]{:S(2)}, u32[]{:S(2)}) collective-permute-start(bf16[1,256,512]{2,1,0:T(8,128)(2,1)S(1)} %get-tuple-element.11), channel_id=1, source_target_pairs={{0,1},{1,2},{2,3},{3,4},{4,5},{5,6},{6,7},{7,8},{8,9},{9,10},{10,1... | collective-permute-start | bytes 786440 | tf_op jit(solution)/shard_map/ppermute | solution.py:419
  100.4 2.0 %collective-permute-start.3 = (bf16[1,256,512]{2,1,0:T(8,128)(2,1)S(1)}, bf16[1,256,512]{2,1,0:T(8,128)(2,1)S(1)}, u32[]{:S(2)}, u32[]{:S(2)}) collective-permute-start(bf16[1,256,512]{2,1,0:T(8,128)(2,1)S(1)} %get-tuple-element.10), channel_id=1, source_target_pairs={{1,0},{2,1},{3,2},{4,3},{5,4},{6,5},{7,6},{8,7},{9,8},{10,9},{11,1... | collective-permute-start | bytes 786440 | tf_op jit(solution)/shard_map/ppermute | solution.py:420
  102.5 1.2 collective-permute-done.2.top_ref
  103.7 4.4 %collective-permute-done.3.bot_ref = bf16[1,256,512]{2,1,0:T(8,128)(2,1)S(1)} collective-permute-done((bf16[1,256,512]{2,1,0:T(8,128)(2,1)S(1)}, bf16[1,256,512]{2,1,0:T(8,128)(2,1)S(1)}, u32[]{:S(2)}, u32[]{:S(2)}) %collective-permute-start.3) | collective-permute-done | bytes 262176 | tf_op jit(solution)/shard_map/ppermute | solution.py:420
  108.1 5.3 %conv_block.3 = bf16[2,256,512]{2,1,0:T(8,128)(2,1)S(1)} custom-call(bf16[1,256,512]{2,1,0:T(8,128)(2,1)S(1)} %collective-permute-done.2.top_ref, bf16[2,256,512]{2,1,0:T(8,128)(2,1)S(1)} %conv_block.2.mid_ref.res_ref, bf16[1,256,512]{2,1,0:T(8,128)(2,1)S(1)} %collective-permute-done.3.bot_ref, bf16[3,3,512,512]{3,2,1,0:T(8,128)(2,1)} %bitcast.42, ...), custom_call_target="tpu_custom_call" | custom-call | flops 2415919104 | bytes 4718592 | tf_op jit(solution)/shard_map/conv_block/pallas_call | solution.py:59
  113.4 1.1 copy.33
  114.5 18.4 %all-to-all-start = ((bf16[16,2,16,512]{3,2,1,0:T(8,128)(2,1)}), bf16[16,2,16,512]{3,2,1,0:T(8,128)(2,1)S(1)}, u32[]{:S(2)}, u32[]{:S(2)}) async-start(bf16[16,2,16,512]{3,2,1,0:T(8,128)(2,1)} %bitcast.45), calls=%async_computation | async-start | bytes 1048576 | tf_op jit(solution)/shard_map/all_to_all | solution.py:499
  132.9 14.1 %all-to-all-done.x_ref = bf16[16,2,16,512]{3,2,1,0:T(8,128)(2,1)S(1)} async-done(((bf16[16,2,16,512]{3,2,1,0:T(8,128)(2,1)}), bf16[16,2,16,512]{3,2,1,0:T(8,128)(2,1)S(1)}, u32[]{:S(2)}, u32[]{:S(2)}) %all-to-all-start) | async-done | bytes 524320 | tf_op jit(solution)/shard_map/all_to_all | solution.py:499
  147.1 1.0 copy-done.8
  148.1 1.0 copy-done.9
  149.1 1.0 copy-done.10
  150.2 9.5 %window_block.1 = bf16[16,2,16,512]{3,2,1,0:T(8,128)(2,1)S(1)} custom-call(bf16[16,2,16,512]{3,2,1,0:T(8,128)(2,1)S(1)} %all-to-all-done.x_ref, bf16[512,512]{1,0:T(8,128)(2,1)S(1)} %copy-done.7, bf16[512,512]{1,0:T(8,128)(2,1)S(1)} %copy-done.8, bf16[512,512]{1,0:T(8,128)(2,1)S(1)} %copy-done.9, bf16[512,512]{1,0:T(8,128)(2,1)S(1)} %copy-done.10, ...), custom_call_target="tpu_custom_call" | custom-call | flops 3489660928 | bytes 6291456 | tf_op jit(solution)/shard_map/window_block/pallas_call | solution.py:121
  159.9 1.0 pad_maximum_fusion
  160.9 4.3 %all-to-all-start.1 = ((bf16[16,48,512]{2,1,0:T(8,128)(2,1)}), bf16[16,48,512]{2,1,0:T(8,128)(2,1)S(1)}, u32[]{:S(2)}, u32[]{:S(2)}) async-start(bf16[16,48,512]{2,1,0:T(8,128)(2,1)} %pad_maximum_fusion), calls=%async_computation.1 | async-start | bytes 1572864 | tf_op jit(solution)/shard_map/all_to_all | solution.py:461
  165.2 19.6 %all-to-all-done.1 = bf16[16,48,512]{2,1,0:T(8,128)(2,1)S(1)} async-done(((bf16[16,48,512]{2,1,0:T(8,128)(2,1)}), bf16[16,48,512]{2,1,0:T(8,128)(2,1)S(1)}, u32[]{:S(2)}, u32[]{:S(2)}) %all-to-all-start.1) | async-done | bytes 786464 | tf_op jit(solution)/shard_map/all_to_all | solution.py:461
  185.1 0.2 copy.34
  185.3 1.1 copy.17
  186.3 0.3 copy_bitcast_fusion.1
  186.6 0.1 pad_maximum_fusion.1.d_ref
  186.8 2.3 %copy-done = bf16[3,3,512,512]{3,2,1,0:T(8,128)(2,1)S(1)} copy-done((bf16[3,3,512,512]{3,2,1,0:T(8,128)(2,1)S(1)}, bf16[3,3,512,512]{3,2,1,0:T(8,128)(2,1)}, u32[]{:S(2)}) %copy-start) | copy-done | bytes 4718616
  189.1 2.6 %up_block.1 = bf16[32,16,512]{2,1,0:T(8,128)(2,1)} custom-call(bf16[3,16,16,512]{3,2,1,0:T(8,128)(2,1)S(1)} %pad_maximum_fusion.1.d_ref, bf16[3,3,512,512]{3,2,1,0:T(8,128)(2,1)S(1)} %copy-done), custom_call_target="tpu_custom_call" | custom-call | flops 1207959552 | bytes 4718592 | tf_op jit(solution)/shard_map/up_block/pallas_call | solution.py:163
  (29 shorter events, 0.5 us)
Async XLA Ops:
  7.2 179.6 %all-gather.2.cloned.1.call-start = ((), (), s32[]{:S(2)}) async-start(), calls=%async_computation.2 | async-start | bytes 5013504 | tf_op jit(solution)/shard_map/all_gather | solution.py:183
  9.0 81.9 %collective-permute-start = (bf16[1,256,512]{2,1,0:T(8,128)(2,1)S(1)}, bf16[1,256,512]{2,1,0:T(8,128)(2,1)S(1)}, u32[]{:S(2)}, u32[]{:S(2)}) collective-permute-start(bf16[1,256,512]{2,1,0:T(8,128)(2,1)S(1)} %get-tuple-element.13), channel_id=1, source_target_pairs={{0,1},{1,2},{2,3},{3,4},{4,5},{5,6},{6,7},{7,8},{8,9},{9,10},{10,1... | collective-permute-start | bytes 786440 | tf_op jit(solution)/shard_map/ppermute | solution.py:419
  12.7 78.2 %collective-permute-start.1 = (bf16[1,256,512]{2,1,0:T(8,128)(2,1)S(1)}, bf16[1,256,512]{2,1,0:T(8,128)(2,1)S(1)}, u32[]{:S(2)}, u32[]{:S(2)}) collective-permute-start(bf16[1,256,512]{2,1,0:T(8,128)(2,1)S(1)} %get-tuple-element.12), channel_id=1, source_target_pairs={{1,0},{2,1},{3,2},{4,3},{5,4},{6,5},{7,6},{8,7},{9,8},{10,9},{11,1... | collective-permute-start | bytes 786440 | tf_op jit(solution)/shard_map/ppermute | solution.py:420
  14.6 1.0 copy-start.2
  15.6 1.0 copy-start.3
  86.5 2.2 %copy-start.4 = (bf16[9,512,512]{2,1,0:T(8,128)(2,1)}, bf16[9,512,512]{2,1,0:T(8,128)(2,1)S(1)}, u32[]{:S(2)}) copy-start(bf16[9,512,512]{2,1,0:T(8,128)(2,1)S(1)} %get-tuple-element.5) | copy-start | bytes 14155780
  88.7 2.2 %copy-start.5 = (bf16[9,512,512]{2,1,0:T(8,128)(2,1)}, bf16[9,512,512]{2,1,0:T(8,128)(2,1)S(1)}, u32[]{:S(2)}) copy-start(bf16[9,512,512]{2,1,0:T(8,128)(2,1)S(1)} %get-tuple-element.4) | copy-start | bytes 14155780
  90.9 1.0 copy-start.1
  97.2 6.5 %collective-permute-start.2 = (bf16[1,256,512]{2,1,0:T(8,128)(2,1)S(1)}, bf16[1,256,512]{2,1,0:T(8,128)(2,1)S(1)}, u32[]{:S(2)}, u32[]{:S(2)}) collective-permute-start(bf16[1,256,512]{2,1,0:T(8,128)(2,1)S(1)} %get-tuple-element.11), channel_id=1, source_target_pairs={{0,1},{1,2},{2,3},{3,4},{4,5},{5,6},{6,7},{7,8},{8,9},{9,10},{10,1... | collective-permute-start | bytes 786440 | tf_op jit(solution)/shard_map/ppermute | solution.py:419
  100.4 7.7 %collective-permute-start.3 = (bf16[1,256,512]{2,1,0:T(8,128)(2,1)S(1)}, bf16[1,256,512]{2,1,0:T(8,128)(2,1)S(1)}, u32[]{:S(2)}, u32[]{:S(2)}) collective-permute-start(bf16[1,256,512]{2,1,0:T(8,128)(2,1)S(1)} %get-tuple-element.10), channel_id=1, source_target_pairs={{1,0},{2,1},{3,2},{4,3},{5,4},{6,5},{7,6},{8,7},{9,8},{10,9},{11,1... | collective-permute-start | bytes 786440 | tf_op jit(solution)/shard_map/ppermute | solution.py:420
  108.1 38.9 %copy-start.7 = (bf16[512,512]{1,0:T(8,128)(2,1)S(1)}, bf16[512,512]{1,0:T(8,128)(2,1)}, u32[]{:S(2)}) copy-start(bf16[512,512]{1,0:T(8,128)(2,1)} %wq_ref.1) | copy-start | bytes 1572868
  113.4 33.6 %copy-start.6 = (bf16[512,2048]{1,0:T(8,128)(2,1)S(1)}, bf16[512,2048]{1,0:T(8,128)(2,1)}, u32[]{:S(2)}) copy-start(bf16[512,2048]{1,0:T(8,128)(2,1)} %wi_ref.1) | copy-start | bytes 6291460
  114.5 32.5 %all-to-all-start = ((bf16[16,2,16,512]{3,2,1,0:T(8,128)(2,1)}), bf16[16,2,16,512]{3,2,1,0:T(8,128)(2,1)S(1)}, u32[]{:S(2)}, u32[]{:S(2)}) async-start(bf16[16,2,16,512]{3,2,1,0:T(8,128)(2,1)} %bitcast.45), calls=%async_computation | async-start | bytes 1048576 | tf_op jit(solution)/shard_map/all_to_all | solution.py:499
  147.1 1.0 copy-start.8
  148.1 1.0 copy-start.9
  149.1 1.0 copy-start.10
  160.9 23.9 %all-to-all-start.1 = ((bf16[16,48,512]{2,1,0:T(8,128)(2,1)}), bf16[16,48,512]{2,1,0:T(8,128)(2,1)S(1)}, u32[]{:S(2)}, u32[]{:S(2)}) async-start(bf16[16,48,512]{2,1,0:T(8,128)(2,1)} %pad_maximum_fusion), calls=%async_computation.1 | async-start | bytes 1572864 | tf_op jit(solution)/shard_map/all_to_all | solution.py:461
  186.8 2.3 %copy-start = (bf16[3,3,512,512]{3,2,1,0:T(8,128)(2,1)S(1)}, bf16[3,3,512,512]{3,2,1,0:T(8,128)(2,1)}, u32[]{:S(2)}) copy-start(bf16[3,3,512,512]{3,2,1,0:T(8,128)(2,1)} %all-gather.2.cloned.1.call-done.k_ref) | copy-start | bytes 14155780
Sparse Core Ops, SparseCore 0:
  10.2 66.9 all-gather.1

commit v3 on v2

--- a/solution.py
+++ b/solution.py
@@ -26,13 +26,23 @@
     return jnp.dot(a, b, preferred_element_type=F32)
 
 
-def conv_body(rows, top_ref, mid_ref, bot_ref, k_ref, res_ref, o_ref, act_ref):
+def conv_body(rows, masked, top_ref, mid_ref, bot_ref, k_ref, res_ref, o_ref, act_ref):
     @pl.when(pl.program_id(0) == 0)
     def _():
         act_ref[0] = gelu(top_ref[0])
         for i in range(rows):
             act_ref[i + 1] = gelu(mid_ref[i])
         act_ref[rows + 1] = gelu(bot_ref[0])
+        if masked:
+            blank = jnp.zeros(act_ref.shape[1:], BF16)
+
+            @pl.when(lax.axis_index("row") == 0)
+            def _():
+                act_ref[0] = blank
+
+            @pl.when(lax.axis_index("row") == lax.axis_size("row") - 1)
+            def _():
+                act_ref[rows + 1] = blank
 
     cols = act_ref.shape[1]
     width = k_ref.shape[3]
@@ -50,14 +60,14 @@
         o_ref[i] = (res_ref[i].astype(F32) + total).astype(BF16)
 
 
-def conv_block(top, mid, bot, kernel, residual):
+def conv_block(top, mid, bot, kernel, residual, masked=False):
     rows, cols, channels = mid.shape
     out_channels = kernel.shape[3]
     width = min(256, out_channels)
     whole = lambda n: pl.BlockSpec((n, cols, channels), lambda b: (0, 0, 0))
     part = pl.BlockSpec((rows, cols, width), lambda b: (0, 0, b))
     return pl.pallas_call(
-        functools.partial(conv_body, rows),
+        functools.partial(conv_body, rows, masked),
         grid=(out_channels // width,),
         in_specs=[
             whole(1),
@@ -69,7 +79,7 @@
         out_specs=part,
         out_shape=jax.ShapeDtypeStruct((rows, cols, out_channels), BF16),
         scratch_shapes=[pltpu.VMEM((rows + 2, cols, channels), BF16)],
-        compiler_params=pltpu.CompilerParams(vmem_limit_bytes=48 << 20),
+        compiler_params=pltpu.CompilerParams(vmem_limit_bytes=60 * 1024 * 1024),
         name="conv_block",
         cost_estimate=pl.CostEstimate(
             flops=18 * rows * cols * channels * out_channels,
@@ -125,7 +135,7 @@
         out_specs=part,
         out_shape=jax.ShapeDtypeStruct(x.shape, BF16),
         scratch_shapes=[pltpu.VMEM((cells, channels), BF16)],
-        compiler_params=pltpu.CompilerParams(vmem_limit_bytes=48 << 20),
+        compiler_params=pltpu.CompilerParams(vmem_limit_bytes=60 * 1024 * 1024),
         name="window_block",
         cost_estimate=pl.CostEstimate(
             flops=2 * bands * cells * (work + 2 * cells * channels),
@@ -169,7 +179,7 @@
         ],
         out_specs=pl.BlockSpec((2 * rows, cols, width), lambda b: (0, 0, b)),
         out_shape=jax.ShapeDtypeStruct((2 * rows, cols, out_channels), BF16),
-        compiler_params=pltpu.CompilerParams(vmem_limit_bytes=48 << 20),
+        compiler_params=pltpu.CompilerParams(vmem_limit_bytes=60 * 1024 * 1024),
         name="up_block",
         cost_estimate=pl.CostEstimate(
             flops=18 * rows * cols * channels * out_channels,
@@ -184,8 +194,10 @@
 
 
 def gather_body(count, nz, *refs):
-    pieces, wholes, owns = refs[:count], refs[count : 2 * count], refs[2 * count : 3 * count]
-    load_sem, keep_sem, zs, zr, ys, yr, xs, xr, cs, cr = refs[3 * count :]
+    pieces, field = refs[:count], refs[count]
+    wholes, before, after = refs[count + 1 : 2 * count + 1], refs[2 * count + 1], refs[2 * count + 2]
+    owns = refs[2 * count + 3 : 3 * count + 3]
+    load_sem, keep_sem, zs, zr, ys, yr, xs, xr, cs, cr, es, er = refs[3 * count + 3 :]
     index, part = lax.axis_index("row"), lax.axis_index("parts")
     core, y, z = index % 2, (index // 2) % 2, index // 4
     parity = part % 2
@@ -284,6 +296,20 @@
         to = device(z, y, 1 - core, part)
         return remote(here, here, cs.at[m, column, slot], cr.at[m, column, slot], to)
 
+    def edge(way):
+        src = field.at[pl.ds(field.shape[0] - 1 if way > 0 else 0, 1)]
+        dst = before if way > 0 else after
+        slot = 0 if way > 0 else 1
+        return remote(src, dst, es.at[slot], er.at[slot], {"parts": part, "row": index + way})
+
+    def edge_arrival(way):
+        dst = before if way > 0 else after
+        slot = 0 if way > 0 else 1
+        return remote(dst, dst, es.at[slot], er.at[slot], {"parts": part, "row": index - way})
+
+    def beside(way):
+        return index < 4 * nz - 1 if way > 0 else index > 0
+
     def when(condition, action):
         if condition is None:
             action()
@@ -313,7 +339,10 @@
     greet(device(z, y, core, part + 1 - 2 * parity))
     for way in (1, -1):
         when(ahead(way), functools.partial(greet, device(z + way, y, core, part)))
-    pl.semaphore_wait(barrier, 3 + jnp.minimum(z, 1) + jnp.minimum(nz - 1 - z, 1))
+        when(beside(way), functools.partial(greet, {"parts": part, "row": index + way}))
+    peers = 3 + jnp.minimum(z, 1) + jnp.minimum(nz - 1 - z, 1)
+    peers = peers + jnp.minimum(index, 1) + jnp.minimum(4 * nz - 1 - index, 1)
+    pl.semaphore_wait(barrier, peers)
 
     loads = [
         pltpu.make_async_copy(pieces[m], owns[m], load_sem.at[m]) for m in range(count)
@@ -329,6 +358,8 @@
         y_copy(m, 0).start()
         c_copy(m, 0, 0).start()
         loads[m].start()
+    for way in (1, -1):
+        when(beside(way), lambda: edge(way).start())
     for m in range(count):
         loads[m].wait()
         keeps[m].start()
@@ -366,6 +397,9 @@
 
                     when(valid(d), from_x)
 
+    for way in (1, -1):
+        when(beside(way), lambda: edge(way).wait_send())
+        when(beside(-way), lambda: edge_arrival(way).wait_recv())
     for m in range(count):
         keeps[m].wait()
         for distance in range(nz):
@@ -385,7 +419,7 @@
                 when(valid(d), finish)
 
 
-def gather_kernels(pieces, collective_id):
+def gather_kernels(pieces, field, collective_id):
     devices = lax.axis_size("row")
     nz = devices // 4
     count = len(pieces)
@@ -396,20 +430,23 @@
     anywhere = pl.BlockSpec(memory_space=pl.ANY)
     outs = pl.pallas_call(
         functools.partial(gather_body, count, nz),
-        in_specs=[anywhere] * count,
-        out_specs=[anywhere] * count,
-        out_shape=[jax.ShapeDtypeStruct((taps, rows * devices, out_channels), BF16)] * count,
+        in_specs=[anywhere] * (count + 1),
+        out_specs=[anywhere] * (count + 2),
+        out_shape=[jax.ShapeDtypeStruct((taps, rows * devices, out_channels), BF16)] * count
+        + [jax.ShapeDtypeStruct((1,) + field.shape[1:], BF16)] * 2,
         scratch_shapes=[pltpu.VMEM((taps, rows, out_channels), BF16)] * count
         + [dma((count,))] * 2
         + [dma((count, slots, 2))] * 2
         + [dma((count, slots))] * 4
-        + [dma((count, 2, slots))] * 2,
+        + [dma((count, 2, slots))] * 2
+        + [dma((2,))] * 2,
         compiler_params=pltpu.CompilerParams(
-            collective_id=collective_id, has_side_effects=True, vmem_limit_bytes=16 << 20
+            collective_id=collective_id, has_side_effects=True, vmem_limit_bytes=60 * 1024 * 1024
         ),
         name="gather_kernels",
-    )(*flat)
-    return [o.reshape(3, 3, rows * devices, out_channels) for o in outs]
+    )(*flat, field)
+    wholes = [o.reshape(3, 3, rows * devices, out_channels) for o in outs[:count]]
+    return wholes, outs[count:]
 
 
 def edge_rows(value):
@@ -473,14 +510,15 @@
     grid_rows, grid_cols, channels = latent.shape
     paired = devices % 4 == 0 and lax.axis_size("parts") % 2 == 0
     if paired and devices <= GRID and conv_first.shape[2] % 32 == 0:
-        kernels = gather_kernels([conv_first, conv_second], 0)
+        kernels, edges = gather_kernels([conv_first, conv_second, conv_up], latent, 0)
+        first, second, up_kernel = kernels
+        current = conv_block(edges[0], latent, edges[1], first, latent, True)
     else:
-        kernels = [whole_kernel(conv_first), whole_kernel(conv_second)]
-    up_kernel = whole_kernel(conv_up)
-    current = latent
-    for kernel in kernels:
-        before, after = edge_rows(current)
-        current = conv_block(before, current, after, kernel, current)
+        first, second, up_kernel = [whole_kernel(k) for k in (conv_first, conv_second, conv_up)]
+        before, after = edge_rows(latent)
+        current = conv_block(before, latent, after, first, latent)
+    before, after = edge_rows(current)
+    current = conv_block(before, current, after, second, current)
 
     step = devices // GRID
     groups = None

time: 199 us -> 174 us (0.87)
  between operations: 14.2 us -> 0.76 us
  local copies, waits for them, and re-layouts: 16.8 us -> 7.54 us
  starting transfers between devices: 33.6 us -> 27.9 us
  Pallas kernels: 92.6 us -> 96.1 us
    unnamed x23 -> x9, local copies, waits for them, and re-layouts: 13 us -> 1.67 us
    ppermute x2 -> x1, starting transfers between devices: 6.91 us -> 1.92 us  [edge_rows(): before = lax.ppermute(value[-1:], 'row', up)]
    ppermute x2 -> x1, waiting for transfers between devices: 4.4 us -> 1.58 us  [edge_rows(): after = lax.ppermute(value[:1], 'row', down)]
    ppermute x2 -> x1, waiting for transfers between devices: 1.25 us -> 3.69 us  [edge_rows(): before = lax.ppermute(value[-1:], 'row', up)]
    pallas_call x1, Pallas kernels: 9.52 us -> 11.5 us  [window_block(): pl.pallas_call(window_body, grid=(bands,), in_specs=[part] + whole, out_s...]
  transfers between devices with their start and end apart: 7 -> 4, of which waited for: 4 -> 4; matrix products, arithmetic and copies ran while one was open for 3% -> 0% of each run, Pallas kernels for 45% -> 0%
where the time goes in v3:
time: 174 us; the launch traced here: 173 us
  Pallas kernels  96.1 us (55%)
  waiting for transfers between devices  39 us (22%)
  starting transfers between devices  27.9 us (16%)
  local copies, waits for them, and re-layouts  7.54 us (4%)
  other arithmetic  2.08 us (1%)
    pallas_call x1, Pallas kernels, gather_kernels(): pl.pallas_call(functools.partial(gather_body, count, nz), in_specs=[anywh...  68 us
    all_to_all x1, waiting for transfers between devices, central_by_windows(): both = lax.all_to_all(both, 'row', split_axis=0, concat_axis=0, tiled=True)  19.6 us
    all_to_all x1, starting transfers between devices, on_device(): exchange(by_column)  19.3 us
    all_to_all x1, waiting for transfers between devices, on_device(): exchange(by_column)  14.1 us
    pallas_call x2, Pallas kernels, conv_block(): pl.pallas_call(functools.partial(conv_body, rows, masked), grid=(out_chan...  12.5 us
    pallas_call x1, Pallas kernels, window_block(): pl.pallas_call(window_body, grid=(bands,), in_specs=[part] + whole, out_s...  11.5 us
    all_to_all x1, starting transfers between devices, central_by_windows(): both = lax.all_to_all(both, 'row', split_axis=0, concat_axis=0, tiled=True)  4.33 us
    pallas_call x1, Pallas kernels, up_block(): pl.pallas_call(up_body, grid=(out_channels // width,), in_specs=[pl.Block...  4.13 us
  transfers between devices with their start and end apart: 4, of which 4 were waited for; matrix products, arithmetic and copies ran while one was open for 0% of the time, Pallas kernels for 0%

profile of v3, /device:TPU:9, one launch (start us, length us, event | category | flops | bytes accessed | tf_op | source)
XLA Modules:
  0.0 173.4 jit_solution(10274846185493793056)
XLA Ops:
  0.6 68.0 %gather_kernels.1 = (bf16[9,512,512]{2,1,0:T(8,128)(2,1)}, bf16[9,512,512]{2,1,0:T(8,128)(2,1)}, bf16[9,512,512]{2,1,0:T(8,128)(2,1)}, bf16[1,256,512]{2,1,0:T(8,128)(2,1)}, bf16[1,256,512]{2,1,0:T(8,128)(2,1)}) custom-call(bf16[9,32,512]{2,1,0:T(8,128)(2,1)} %bitcast.51, bf16[9,32,512]{2,1,0:T(8,128)(2,1)} %bitcast.52, bf16[9,32,512]{2,1,0:T(8,128)(2,1)} %bitcast.53, ...), custom_call_target="tpu_custom_call" | custom-call | tf_op jit(solution)/shard_map/gather_kernels/pallas_call | solution.py:431
  68.6 6.2 %conv_block.2.mid_ref.res_ref = bf16[2,256,512]{2,1,0:T(8,128)(2,1)} custom-call(bf16[1,256,512]{2,1,0:T(8,128)(2,1)} %get-tuple-element.7.top_ref, bf16[2,256,512]{2,1,0:T(8,128)(2,1)} %res_ref.1, bf16[1,256,512]{2,1,0:T(8,128)(2,1)} %get-tuple-element.8.bot_ref, bf16[3,3,512,512]{3,2,1,0:T(8,128)(2,1)} %bitcast.55, bf16[2,256,512]{2,1,0:T(8,128)(2,1)} %res_ref.1), custom_call_target="tpu_custom_call" | custom-call | flops 2415919104 | bytes 4718592 | tf_op jit(solution)/shard_map/conv_block/pallas_call | solution.py:69
  74.9 1.1 fusion.3
  75.9 1.9 %collective-permute-start = (bf16[1,256,512]{2,1,0:T(8,128)(2,1)S(1)}, bf16[1,256,512]{2,1,0:T(8,128)(2,1)S(1)}, u32[]{:S(2)}, u32[]{:S(2)}) collective-permute-start(bf16[1,256,512]{2,1,0:T(8,128)(2,1)S(1)} %get-tuple-element.17), channel_id=1, source_target_pairs={{0,1},{1,2},{2,3},{3,4},{4,5},{5,6},{6,7},{7,8},{8,9},{9,10},{10,1... | collective-permute-start | bytes 786440 | tf_op jit(solution)/shard_map/ppermute | solution.py:456
  77.9 2.4 %collective-permute-start.1 = (bf16[1,256,512]{2,1,0:T(8,128)(2,1)S(1)}, bf16[1,256,512]{2,1,0:T(8,128)(2,1)S(1)}, u32[]{:S(2)}, u32[]{:S(2)}) collective-permute-start(bf16[1,256,512]{2,1,0:T(8,128)(2,1)S(1)} %get-tuple-element.16), channel_id=1, source_target_pairs={{1,0},{2,1},{3,2},{4,3},{5,4},{6,5},{7,6},{8,7},{9,8},{10,9},{11,1... | collective-permute-start | bytes 786440 | tf_op jit(solution)/shard_map/ppermute | solution.py:457
  80.3 3.7 %collective-permute-done.top_ref = bf16[1,256,512]{2,1,0:T(8,128)(2,1)S(1)} collective-permute-done((bf16[1,256,512]{2,1,0:T(8,128)(2,1)S(1)}, bf16[1,256,512]{2,1,0:T(8,128)(2,1)S(1)}, u32[]{:S(2)}, u32[]{:S(2)}) %collective-permute-start) | collective-permute-done | bytes 262176 | tf_op jit(solution)/shard_map/ppermute | solution.py:456
  84.0 0.0 copy-start.2
  84.0 1.6 collective-permute-done.1.bot_ref
  85.6 0.0 copy-start.3
  85.6 0.0 copy-done.2
  85.6 0.7 copy-done.3
  86.3 6.2 %conv_block.3 = bf16[2,256,512]{2,1,0:T(8,128)(2,1)} custom-call(bf16[1,256,512]{2,1,0:T(8,128)(2,1)} %copy-done.2, bf16[2,256,512]{2,1,0:T(8,128)(2,1)} %conv_block.2.mid_ref.res_ref, bf16[1,256,512]{2,1,0:T(8,128)(2,1)} %copy-done.3, bf16[3,3,512,512]{3,2,1,0:T(8,128)(2,1)} %bitcast.54, bf16[2,256,512]{2,1,0:T(8,128)(2,1)} %conv_block.2.mid_ref.res_ref), custom_call_target="tpu_custom_call" | custom-call | flops 2415919104 | bytes 4718592 | tf_op jit(solution)/shard_map/conv_block/pallas_call | solution.py:69
  92.5 2.1 %copy.33 = bf16[2,16,16,512]{3,1,0,2:T(8,128)(2,1)} copy(bf16[2,16,16,512]{3,2,1,0:T(8,128)(2,1)} %bitcast.50) | data formatting | bytes 1048576 | tf_op jit(solution)/shard_map/reshape | solution.py:535
  94.6 19.3 %all-to-all-start = ((bf16[16,2,16,512]{3,2,1,0:T(8,128)(2,1)}), bf16[16,2,16,512]{3,2,1,0:T(8,128)(2,1)S(1)}, u32[]{:S(2)}, u32[]{:S(2)}) async-start(bf16[16,2,16,512]{3,2,1,0:T(8,128)(2,1)} %bitcast.37), calls=%async_computation | async-start | bytes 1048576 | tf_op jit(solution)/shard_map/all_to_all | solution.py:537
  113.9 14.1 %all-to-all-done.x_ref = bf16[16,2,16,512]{3,2,1,0:T(8,128)(2,1)S(1)} async-done(((bf16[16,2,16,512]{3,2,1,0:T(8,128)(2,1)}), bf16[16,2,16,512]{3,2,1,0:T(8,128)(2,1)S(1)}, u32[]{:S(2)}, u32[]{:S(2)}) %all-to-all-start) | async-done | bytes 524320 | tf_op jit(solution)/shard_map/all_to_all | solution.py:537
  128.0 0.0 copy-start.1
  128.0 0.8 copy-done.1
  128.8 11.5 %window_block.1 = bf16[16,2,16,512]{3,2,1,0:T(8,128)(2,1)} custom-call(bf16[16,2,16,512]{3,2,1,0:T(8,128)(2,1)} %copy-done.1, bf16[512,512]{1,0:T(8,128)(2,1)} %wq_ref.1, bf16[512,512]{1,0:T(8,128)(2,1)} %wk_ref.1, bf16[512,512]{1,0:T(8,128)(2,1)} %wv_ref.1, bf16[512,512]{1,0:T(8,128)(2,1)} %wo_ref.1, bf16[512,2048]{1,0:T(8,128)(2,1)} %wi_ref.1, ...), custom_call_target="tpu_custom_call" | custom-call | flops 3489660928 | bytes 6291456 | tf_op jit(solution)/shard_map/window_block/pallas_call | solution.py:131
  140.4 0.0 copy-start
  140.4 1.1 slice.63
  141.5 0.1 select_bitcast_fusion.1
  141.6 0.0 copy-done
  141.6 1.0 pad_maximum_fusion
  142.6 4.3 %all-to-all-start.1 = ((bf16[16,48,512]{2,1,0:T(8,128)(2,1)}), bf16[16,48,512]{2,1,0:T(8,128)(2,1)S(1)}, u32[]{:S(2)}, u32[]{:S(2)}) async-start(bf16[16,48,512]{2,1,0:T(8,128)(2,1)} %pad_maximum_fusion), calls=%async_computation.1 | async-start | bytes 1572864 | tf_op jit(solution)/shard_map/all_to_all | solution.py:498
  146.9 19.6 %all-to-all-done.1 = bf16[16,48,512]{2,1,0:T(8,128)(2,1)S(1)} async-done(((bf16[16,48,512]{2,1,0:T(8,128)(2,1)}), bf16[16,48,512]{2,1,0:T(8,128)(2,1)S(1)}, u32[]{:S(2)}, u32[]{:S(2)}) %all-to-all-start.1) | async-done | bytes 786464 | tf_op jit(solution)/shard_map/all_to_all | solution.py:498
  166.6 0.1 fusion.4
  166.7 0.2 copy.34
  166.9 1.1 copy.17
  168.0 0.3 copy_bitcast_fusion.1
  168.3 1.0 pad_maximum_fusion.1.d_ref
  169.3 4.1 %up_block.1 = bf16[32,16,512]{2,1,0:T(8,128)(2,1)} custom-call(bf16[3,16,16,512]{3,2,1,0:T(8,128)(2,1)} %pad_maximum_fusion.1.d_ref, bf16[3,3,512,512]{3,2,1,0:T(8,128)(2,1)} %bitcast.40), custom_call_target="tpu_custom_call" | custom-call | flops 1207959552 | bytes 4718592 | tf_op jit(solution)/shard_map/up_block/pallas_call | solution.py:173
  (8 shorter events, 0.2 us)
Async XLA Ops:
  75.9 8.0 %collective-permute-start = (bf16[1,256,512]{2,1,0:T(8,128)(2,1)S(1)}, bf16[1,256,512]{2,1,0:T(8,128)(2,1)S(1)}, u32[]{:S(2)}, u32[]{:S(2)}) collective-permute-start(bf16[1,256,512]{2,1,0:T(8,128)(2,1)S(1)} %get-tuple-element.17), channel_id=1, source_target_pairs={{0,1},{1,2},{2,3},{3,4},{4,5},{5,6},{6,7},{7,8},{8,9},{9,10},{10,1... | collective-permute-start | bytes 786440 | tf_op jit(solution)/shard_map/ppermute | solution.py:456
  77.9 7.7 %collective-permute-start.1 = (bf16[1,256,512]{2,1,0:T(8,128)(2,1)S(1)}, bf16[1,256,512]{2,1,0:T(8,128)(2,1)S(1)}, u32[]{:S(2)}, u32[]{:S(2)}) collective-permute-start(bf16[1,256,512]{2,1,0:T(8,128)(2,1)S(1)} %get-tuple-element.16), channel_id=1, source_target_pairs={{1,0},{2,1},{3,2},{4,3},{5,4},{6,5},{7,6},{8,7},{9,8},{10,9},{11,1... | collective-permute-start | bytes 786440 | tf_op jit(solution)/shard_map/ppermute | solution.py:457
  84.0 1.6 copy-start.2
  85.6 0.7 copy-start.3
  94.6 33.4 %all-to-all-start = ((bf16[16,2,16,512]{3,2,1,0:T(8,128)(2,1)}), bf16[16,2,16,512]{3,2,1,0:T(8,128)(2,1)S(1)}, u32[]{:S(2)}, u32[]{:S(2)}) async-start(bf16[16,2,16,512]{3,2,1,0:T(8,128)(2,1)} %bitcast.37), calls=%async_computation | async-start | bytes 1048576 | tf_op jit(solution)/shard_map/all_to_all | solution.py:537
  128.0 0.8 copy-start.1
  140.4 1.2 copy-start
  142.6 23.9 %all-to-all-start.1 = ((bf16[16,48,512]{2,1,0:T(8,128)(2,1)}), bf16[16,48,512]{2,1,0:T(8,128)(2,1)S(1)}, u32[]{:S(2)}, u32[]{:S(2)}) async-start(bf16[16,48,512]{2,1,0:T(8,128)(2,1)} %pad_maximum_fusion), calls=%async_computation.1 | async-start | bytes 1572864 | tf_op jit(solution)/shard_map/all_to_all | solution.py:498

commit v4 on v3

--- a/solution.py
+++ b/solution.py
@@ -266,17 +266,23 @@
         slot = d + zero
         return remote(here, here, ys.at[m, slot], yr.at[m, slot], device(z, 1 - y, core, part))
 
-    def x_copy(m, d):
-        here = place(wholes[m], z - d, 1 - y, 0)
+    def x_move(m, column, d, t):
+        here = place(wholes[m], z - d, y if column == 0 else 1 - y, t)
         slot = d + zero
         to = device(z, y, core, part + 1 - 2 * parity)
-        return remote(here, here, xs.at[m, slot], xr.at[m, slot], to)
-
-    def x_arrival(m, d):
-        here = place(wholes[m], z - d, 1 - y, 1)
-        slot = d + zero
-        to = device(z, y, core, part + 1 - 2 * parity)
-        return remote(here, here, xs.at[m, slot], xr.at[m, slot], to)
+        return remote(here, here, xs.at[m, column, slot], xr.at[m, column, slot], to)
+
+    def x_copy(m, d, column=1):
+        return x_move(m, column, d, 0)
+
+    def x_arrival(m, d, column=1):
+        return x_move(m, column, d, 1)
+
+    def lean(m):
+        return m % 3 == 1
+
+    def halves(m):
+        return (0,) if lean(m) else (0, 1)
 
     def c_copy(m, column, d):
         slot = d + zero
@@ -352,7 +358,7 @@
         for m in range(count)
     ]
     for m in range(count):
-        for t in range(2):
+        for t in halves(m):
             for way in (1, -1):
                 when(ahead(way), lambda: z_copy(m, 0, t, way).start())
         y_copy(m, 0).start()
@@ -371,15 +377,26 @@
                     way = 1 if d > 0 else -1
 
                     def from_z():
-                        for t in range(2):
+                        for t in halves(m):
                             z_arrival(m, d, t).wait_recv()
                             if distance < nz - 1:
                                 when(ahead(way), lambda: z_copy(m, d, t, way).start())
                             if t == 0:
                                 y_copy(m, d).start()
+                        if lean(m):
+                            x_copy(m, d, 0).start()
+                        else:
+                            c_copy(m, 0, d).start()
+
+                    when(valid(d), from_z)
+            if lean(m) and 1 <= distance - 1 < nz:
+                for d in both(distance - 1):
+
+                    def from_part():
+                        x_arrival(m, d, 0).wait_recv()
                         c_copy(m, 0, d).start()
 
-                    when(valid(d), from_z)
+                    when(valid(d), from_part)
             if distance - 1 < nz:
                 for d in both(distance - 1):
 
@@ -408,12 +425,14 @@
                 def finish():
                     y_copy(m, d).wait_send()
                     x_copy(m, d).wait_send()
+                    if lean(m) and distance > 0:
+                        x_copy(m, d, 0).wait_send()
                     for column in range(2):
                         c_copy(m, column, d).wait_send()
                         c_arrival(m, column, d).wait_recv()
                     for way in (1, -1):
                         if d * way >= 0 and distance < nz - 1:
-                            for t in range(2):
+                            for t in halves(m):
                                 when(ahead(way), lambda: z_copy(m, d, t, way).wait_send())
 
                 when(valid(d), finish)
@@ -437,8 +456,8 @@
         scratch_shapes=[pltpu.VMEM((taps, rows, out_channels), BF16)] * count
         + [dma((count,))] * 2
         + [dma((count, slots, 2))] * 2
-        + [dma((count, slots))] * 4
-        + [dma((count, 2, slots))] * 2
+        + [dma((count, slots))] * 2
+        + [dma((count, 2, slots))] * 4
         + [dma((2,))] * 2,
         compiler_params=pltpu.CompilerParams(
             collective_id=collective_id, has_side_effects=True, vmem_limit_bytes=60 * 1024 * 1024

time: 174 us -> 166 us (0.954)
  starting transfers between devices: 27.9 us -> 19.7 us
  waiting for transfers between devices: 39 us -> 42.3 us
  Pallas kernels: 96.1 us -> 93.6 us
    all_to_all x1, starting transfers between devices: 19.3 us -> 10.3 us  [on_device(): exchange(by_column)]
    ppermute x1, waiting for transfers between devices: 1.58 us -> 7.2 us  [edge_rows(): after = lax.ppermute(value[:1], 'row', down)]
    pallas_call x1, Pallas kernels: 68 us -> 65.4 us  [gather_kernels(): pl.pallas_call(functools.partial(gather_body, count, nz), in_specs=[anywh...]
    ppermute x1, waiting for transfers between devices: 3.69 us -> 1.37 us  [edge_rows(): before = lax.ppermute(value[-1:], 'row', up)]
where the time goes in v4:
time: 166 us
  Pallas kernels  93.6 us (56%)
  waiting for transfers between devices  42.3 us (25%)
  starting transfers between devices  19.7 us (12%)
  local copies, waits for them, and re-layouts  7.54 us (5%)
  other arithmetic  2.08 us (1%)
    pallas_call x1, Pallas kernels, gather_kernels(): pl.pallas_call(functools.partial(gather_body, count, nz), in_specs=[anywh...  65.4 us
    all_to_all x1, waiting for transfers between devices, central_by_windows(): both = lax.all_to_all(both, 'row', split_axis=0, concat_axis=0, tiled=True)  19.6 us
    all_to_all x1, waiting for transfers between devices, on_device(): exchange(by_column)  14.1 us
    pallas_call x2, Pallas kernels, conv_block(): pl.pallas_call(functools.partial(conv_body, rows, masked), grid=(out_chan...  12.5 us
    pallas_call x1, Pallas kernels, window_block(): pl.pallas_call(window_body, grid=(bands,), in_specs=[part] + whole, out_s...  11.5 us
    all_to_all x1, starting transfers between devices, on_device(): exchange(by_column)  10.3 us
    ppermute x1, waiting for transfers between devices, edge_rows(): after = lax.ppermute(value[:1], 'row', down)  7.2 us
    all_to_all x1, starting transfers between devices, central_by_windows(): both = lax.all_to_all(both, 'row', split_axis=0, concat_axis=0, tiled=True)  4.32 us
  transfers between devices with their start and end apart: 4, of which 4 were waited for; matrix products, arithmetic and copies ran while one was open for 0% of the time, Pallas kernels for 0%

profile of v4, /device:TPU:9, one launch (start us, length us, event | category | flops | bytes accessed | tf_op | source)
XLA Modules:
  0.0 165.9 jit_solution(14103840782097454052)
XLA Ops:
  0.6 65.4 %gather_kernels.1 = (bf16[9,512,512]{2,1,0:T(8,128)(2,1)}, bf16[9,512,512]{2,1,0:T(8,128)(2,1)}, bf16[9,512,512]{2,1,0:T(8,128)(2,1)}, bf16[1,256,512]{2,1,0:T(8,128)(2,1)}, bf16[1,256,512]{2,1,0:T(8,128)(2,1)}) custom-call(bf16[9,32,512]{2,1,0:T(8,128)(2,1)} %bitcast.51, bf16[9,32,512]{2,1,0:T(8,128)(2,1)} %bitcast.52, bf16[9,32,512]{2,1,0:T(8,128)(2,1)} %bitcast.53, ...), custom_call_target="tpu_custom_call" | custom-call | tf_op jit(solution)/shard_map/gather_kernels/pallas_call | solution.py:450
  66.1 6.2 %conv_block.2.mid_ref.res_ref = bf16[2,256,512]{2,1,0:T(8,128)(2,1)} custom-call(bf16[1,256,512]{2,1,0:T(8,128)(2,1)} %get-tuple-element.7.top_ref, bf16[2,256,512]{2,1,0:T(8,128)(2,1)} %res_ref.1, bf16[1,256,512]{2,1,0:T(8,128)(2,1)} %get-tuple-element.8.bot_ref, bf16[3,3,512,512]{3,2,1,0:T(8,128)(2,1)} %bitcast.55, bf16[2,256,512]{2,1,0:T(8,128)(2,1)} %res_ref.1), custom_call_target="tpu_custom_call" | custom-call | flops 2415919104 | bytes 4718592 | tf_op jit(solution)/shard_map/conv_block/pallas_call | solution.py:69
  72.3 1.1 fusion.3
  73.4 3.2 %collective-permute-start = (bf16[1,256,512]{2,1,0:T(8,128)(2,1)S(1)}, bf16[1,256,512]{2,1,0:T(8,128)(2,1)S(1)}, u32[]{:S(2)}, u32[]{:S(2)}) collective-permute-start(bf16[1,256,512]{2,1,0:T(8,128)(2,1)S(1)} %get-tuple-element.17), channel_id=1, source_target_pairs={{0,1},{1,2},{2,3},{3,4},{4,5},{5,6},{6,7},{7,8},{8,9},{9,10},{10,1... | collective-permute-start | bytes 786440 | tf_op jit(solution)/shard_map/ppermute | solution.py:475
  76.6 1.9 %collective-permute-start.1 = (bf16[1,256,512]{2,1,0:T(8,128)(2,1)S(1)}, bf16[1,256,512]{2,1,0:T(8,128)(2,1)S(1)}, u32[]{:S(2)}, u32[]{:S(2)}) collective-permute-start(bf16[1,256,512]{2,1,0:T(8,128)(2,1)S(1)} %get-tuple-element.16), channel_id=1, source_target_pairs={{1,0},{2,1},{3,2},{4,3},{5,4},{6,5},{7,6},{8,7},{9,8},{10,9},{11,1... | collective-permute-start | bytes 786440 | tf_op jit(solution)/shard_map/ppermute | solution.py:476
  78.5 1.4 collective-permute-done.top_ref
  79.9 0.0 copy-start.2
  79.9 7.2 %collective-permute-done.1.bot_ref = bf16[1,256,512]{2,1,0:T(8,128)(2,1)S(1)} collective-permute-done((bf16[1,256,512]{2,1,0:T(8,128)(2,1)S(1)}, bf16[1,256,512]{2,1,0:T(8,128)(2,1)S(1)}, u32[]{:S(2)}, u32[]{:S(2)}) %collective-permute-start.1) | collective-permute-done | bytes 262176 | tf_op jit(solution)/shard_map/ppermute | solution.py:476
  87.1 0.0 copy-start.3
  87.1 0.0 copy-done.2
  87.1 0.7 copy-done.3
  87.8 6.2 %conv_block.3 = bf16[2,256,512]{2,1,0:T(8,128)(2,1)} custom-call(bf16[1,256,512]{2,1,0:T(8,128)(2,1)} %copy-done.2, bf16[2,256,512]{2,1,0:T(8,128)(2,1)} %conv_block.2.mid_ref.res_ref, bf16[1,256,512]{2,1,0:T(8,128)(2,1)} %copy-done.3, bf16[3,3,512,512]{3,2,1,0:T(8,128)(2,1)} %bitcast.54, bf16[2,256,512]{2,1,0:T(8,128)(2,1)} %conv_block.2.mid_ref.res_ref), custom_call_target="tpu_custom_call" | custom-call | flops 2415919104 | bytes 4718592 | tf_op jit(solution)/shard_map/conv_block/pallas_call | solution.py:69
  94.0 2.1 %copy.33 = bf16[2,16,16,512]{3,1,0,2:T(8,128)(2,1)} copy(bf16[2,16,16,512]{3,2,1,0:T(8,128)(2,1)} %bitcast.50) | data formatting | bytes 1048576 | tf_op jit(solution)/shard_map/reshape | solution.py:554
  96.1 10.3 %all-to-all-start = ((bf16[16,2,16,512]{3,2,1,0:T(8,128)(2,1)}), bf16[16,2,16,512]{3,2,1,0:T(8,128)(2,1)S(1)}, u32[]{:S(2)}, u32[]{:S(2)}) async-start(bf16[16,2,16,512]{3,2,1,0:T(8,128)(2,1)} %bitcast.37), calls=%async_computation | async-start | bytes 1048576 | tf_op jit(solution)/shard_map/all_to_all | solution.py:556
  106.4 14.1 %all-to-all-done.x_ref = bf16[16,2,16,512]{3,2,1,0:T(8,128)(2,1)S(1)} async-done(((bf16[16,2,16,512]{3,2,1,0:T(8,128)(2,1)}), bf16[16,2,16,512]{3,2,1,0:T(8,128)(2,1)S(1)}, u32[]{:S(2)}, u32[]{:S(2)}) %all-to-all-start) | async-done | bytes 524320 | tf_op jit(solution)/shard_map/all_to_all | solution.py:556
  120.5 0.0 copy-start.1
  120.5 0.8 copy-done.1
  121.3 11.5 %window_block.1 = bf16[16,2,16,512]{3,2,1,0:T(8,128)(2,1)} custom-call(bf16[16,2,16,512]{3,2,1,0:T(8,128)(2,1)} %copy-done.1, bf16[512,512]{1,0:T(8,128)(2,1)} %wq_ref.1, bf16[512,512]{1,0:T(8,128)(2,1)} %wk_ref.1, bf16[512,512]{1,0:T(8,128)(2,1)} %wv_ref.1, bf16[512,512]{1,0:T(8,128)(2,1)} %wo_ref.1, bf16[512,2048]{1,0:T(8,128)(2,1)} %wi_ref.1, ...), custom_call_target="tpu_custom_call" | custom-call | flops 3489660928 | bytes 6291456 | tf_op jit(solution)/shard_map/window_block/pallas_call | solution.py:131
  132.9 0.0 copy-start
  132.9 1.1 slice.63
  134.0 0.1 select_bitcast_fusion.1
  134.1 0.0 copy-done
  134.1 1.0 pad_maximum_fusion
  135.1 4.3 %all-to-all-start.1 = ((bf16[16,48,512]{2,1,0:T(8,128)(2,1)}), bf16[16,48,512]{2,1,0:T(8,128)(2,1)S(1)}, u32[]{:S(2)}, u32[]{:S(2)}) async-start(bf16[16,48,512]{2,1,0:T(8,128)(2,1)} %pad_maximum_fusion), calls=%async_computation.1 | async-start | bytes 1572864 | tf_op jit(solution)/shard_map/all_to_all | solution.py:517
  139.4 19.6 %all-to-all-done.1 = bf16[16,48,512]{2,1,0:T(8,128)(2,1)S(1)} async-done(((bf16[16,48,512]{2,1,0:T(8,128)(2,1)}), bf16[16,48,512]{2,1,0:T(8,128)(2,1)S(1)}, u32[]{:S(2)}, u32[]{:S(2)}) %all-to-all-start.1) | async-done | bytes 786464 | tf_op jit(solution)/shard_map/all_to_all | solution.py:517
  159.1 0.1 fusion.4
  159.2 0.2 copy.34
  159.4 1.1 copy.17
  160.5 0.3 copy_bitcast_fusion.1
  160.8 1.0 pad_maximum_fusion.1.d_ref
  161.8 4.1 %up_block.1 = bf16[32,16,512]{2,1,0:T(8,128)(2,1)} custom-call(bf16[3,16,16,512]{3,2,1,0:T(8,128)(2,1)} %pad_maximum_fusion.1.d_ref, bf16[3,3,512,512]{3,2,1,0:T(8,128)(2,1)} %bitcast.40), custom_call_target="tpu_custom_call" | custom-call | flops 1207959552 | bytes 4718592 | tf_op jit(solution)/shard_map/up_block/pallas_call | solution.py:173
  (8 shorter events, 0.2 us)
Async XLA Ops:
  73.4 6.5 %collective-permute-start = (bf16[1,256,512]{2,1,0:T(8,128)(2,1)S(1)}, bf16[1,256,512]{2,1,0:T(8,128)(2,1)S(1)}, u32[]{:S(2)}, u32[]{:S(2)}) collective-permute-start(bf16[1,256,512]{2,1,0:T(8,128)(2,1)S(1)} %get-tuple-element.17), channel_id=1, source_target_pairs={{0,1},{1,2},{2,3},{3,4},{4,5},{5,6},{6,7},{7,8},{8,9},{9,10},{10,1... | collective-permute-start | bytes 786440 | tf_op jit(solution)/shard_map/ppermute | solution.py:475
  76.6 10.5 %collective-permute-start.1 = (bf16[1,256,512]{2,1,0:T(8,128)(2,1)S(1)}, bf16[1,256,512]{2,1,0:T(8,128)(2,1)S(1)}, u32[]{:S(2)}, u32[]{:S(2)}) collective-permute-start(bf16[1,256,512]{2,1,0:T(8,128)(2,1)S(1)} %get-tuple-element.16), channel_id=1, source_target_pairs={{1,0},{2,1},{3,2},{4,3},{5,4},{6,5},{7,6},{8,7},{9,8},{10,9},{11,1... | collective-permute-start | bytes 786440 | tf_op jit(solution)/shard_map/ppermute | solution.py:476
  79.9 7.2 %copy-start.2 = (bf16[1,256,512]{2,1,0:T(8,128)(2,1)}, bf16[1,256,512]{2,1,0:T(8,128)(2,1)S(1)}, u32[]{:S(2)}) copy-start(bf16[1,256,512]{2,1,0:T(8,128)(2,1)S(1)} %collective-permute-done.top_ref) | copy-start | bytes 786436
  87.1 0.7 copy-start.3
  96.1 24.4 %all-to-all-start = ((bf16[16,2,16,512]{3,2,1,0:T(8,128)(2,1)}), bf16[16,2,16,512]{3,2,1,0:T(8,128)(2,1)S(1)}, u32[]{:S(2)}, u32[]{:S(2)}) async-start(bf16[16,2,16,512]{3,2,1,0:T(8,128)(2,1)} %bitcast.37), calls=%async_computation | async-start | bytes 1048576 | tf_op jit(solution)/shard_map/all_to_all | solution.py:556
  120.5 0.8 copy-start.1
  132.9 1.2 copy-start
  135.1 23.9 %all-to-all-start.1 = ((bf16[16,48,512]{2,1,0:T(8,128)(2,1)}), bf16[16,48,512]{2,1,0:T(8,128)(2,1)S(1)}, u32[]{:S(2)}, u32[]{:S(2)}) async-start(bf16[16,48,512]{2,1,0:T(8,128)(2,1)} %pad_maximum_fusion), calls=%async_computation.1 | async-start | bytes 1572864 | tf_op jit(solution)/shard_map/all_to_all | solution.py:517
